TPU v7x, 32 devices: a whole 2x2x4 slice. The times are simulated.
32 devices in a mesh: parts: 2 (over y), tm: 4 (over z), space: 2 (over x), spin: 2 (over core).
Axes of the slice: x: 2, y: 2, z: 4, core: 2. Of those that a mesh axis runs over, the one named last changes fastest.
Arguments:
- eigenvectors: float32 [2, 8, 3, 512, 256], P(None, ('parts', 'tm'), None, ('space', 'spin')), parts along dimension 1, may hold values from -0.25 to 0.25
- displaced: float32 [2, 3, 8, 3, 512, 256], P(None, None, ('parts', 'tm'), None, ('space', 'spin')), parts along dimension 2, may hold values from -0.25 to 0.25
- perambulators: float32 [2, 8, 4, 256, 256], P(None, 'parts', 'spin', 'space', 'tm'), parts along dimension 1, may hold values from -6 to 6
- gamma_values: float32 [2, 4, 4, 4], replicated, may hold values from -4 to 4
- spin_pattern: int32 [4, 4, 4], replicated, may hold values 0 or 1
- directions: int32 [4], replicated, may hold values from 0 to 2, as said below
- momenta: int32 [4], replicated, may hold values from 0 to 3
Outputs:
- products: float32 [2, 4, 8, 4, 256, 256], P(None, None, ('parts', 'tm'), 'spin', 'space'), parts along dimension 2
There are 2 independent parts, one for each index of `parts`. A program takes and returns all parts, laid end to end along the dimension named above; an argument that names none is the same for every part. Nothing has to cross between parts.
Inputs may be any that keep to these rules, and one draw needn't show every extreme that they name: Every one of the 3 directions is named by some operator.
All inputs are finite; a program needn't handle non-finite values.
Results may differ from a plain program's by a relative error of at most 0.0001.
Values sent between devices are 32-bit elements; how exact they have to be, the bound alone decides.
No kernel may reach another device: no remote copies, remote signals or barrier semaphores. Data moves between devices by JAX's collectives and lax.ppermute only.
A program may use at most 64 MiB of HBM per device.

v0:
```python
import math

import jax
import jax.numpy as jnp
from jax import lax
from jax.sharding import PartitionSpec as P

highest = lax.Precision.HIGHEST


def local(eigenvectors, displaced, perambulators, gamma_values, spin_pattern, directions, momenta):
    time_dev = eigenvectors.shape[1]
    sites_dev = eigenvectors.shape[3]
    width = eigenvectors.shape[4]
    op_count = gamma_values.shape[1]
    spin_count = gamma_values.shape[2]
    sites_total = lax.axis_size(("space", "spin")) * sites_dev
    plane_sites = 2 * sites_dev
    extent = sites_total // plane_sites
    rows_dev = width // lax.axis_size("space")
    positions = lax.axis_index(("space", "spin")) * sites_dev + jnp.arange(
        sites_dev, dtype=jnp.int32
    )
    third = positions // plane_sites
    angles = (momenta[:, None] * third[None, :] % extent).astype(jnp.float32) * (
        2.0 * math.pi / extent
    )
    cosine = jnp.cos(angles)
    sine = jnp.sin(angles)
    tslice = 0
    lefts = [eigenvectors[:, tslice].reshape(-1, width)]
    columns = []
    for operator in range(op_count):
        moved = lax.dynamic_index_in_dim(displaced, directions[operator], 1, keepdims=False)[
            :, tslice
        ]
        cos_row = cosine[operator][:, None]
        sin_row = sine[operator][:, None]
        real_w = cos_row * moved[0] + sin_row * moved[1]
        imag_w = cos_row * moved[1] - sin_row * moved[0]
        block = jnp.concatenate(
            [jnp.stack([real_w, imag_w]), jnp.stack([imag_w, -real_w])], axis=-1
        )
        columns.append(block.reshape(-1, 2 * width))
    rights = [jnp.concatenate(columns, axis=1)]
    tslice = 0
    left_rows = lefts[tslice]
    pieces = lax.dot_general(
        left_rows,
        rights[tslice],
        (((0,), (0,)), ((), ())),
        precision=highest,
        preferred_element_type=jnp.float32,
    )
    quarter = lax.psum_scatter(pieces, ("space", "spin"), scatter_dimension=0, tiled=True)
    own_rows = lax.all_gather(quarter, "spin", axis=0, tiled=True)
    elementals = own_rows.reshape(rows_dev, time_dev, op_count, 2, width)
    spin_matrix = gamma_values * spin_pattern.astype(jnp.float32)[None]
    sink_dev = spin_count // lax.axis_size("spin")
    spin_rows = lax.dynamic_slice_in_dim(
        spin_matrix, lax.axis_index("spin") * sink_dev, sink_dev, 2
    )
    arrived = lax.all_to_all(perambulators, "tm", split_axis=1, concat_axis=4, tiled=True)
    arrived = lax.all_gather(arrived, "spin", axis=2, tiled=True)
    piece = lax.all_gather(arrived, "space", axis=3, tiled=True)
    real_q = jnp.einsum("oab,tbls->otals", spin_rows[0], piece[0], precision=highest) - jnp.einsum(
        "oab,tbls->otals", spin_rows[1], piece[1], precision=highest
    )
    imag_q = jnp.einsum("oab,tbls->otals", spin_rows[0], piece[1], precision=highest) + jnp.einsum(
        "oab,tbls->otals", spin_rows[1], piece[0], precision=highest
    )
    block = elementals
    real_e = block[:, :, :, 0]
    imag_e = block[:, :, :, 1]
    real_r = jnp.einsum("ktol,otals->otaks", real_e, real_q, precision=highest) - jnp.einsum(
        "ktol,otals->otaks", imag_e, imag_q, precision=highest
    )
    imag_r = jnp.einsum("ktol,otals->otaks", real_e, imag_q, precision=highest) + jnp.einsum(
        "ktol,otals->otaks", imag_e, real_q, precision=highest
    )
    return jnp.stack([real_r, imag_r])


def solution(mesh):
    in_specs = (
        P(None, ("parts", "tm"), None, ("space", "spin"), None),
        P(None, None, ("parts", "tm"), None, ("space", "spin"), None),
        P(None, "parts", "spin", "space", "tm"),
        P(),
        P(),
        P(),
        P(),
    )
    out_specs = P(None, None, ("parts", "tm"), "spin", "space", None)
    return jax.shard_map(local, mesh=mesh, in_specs=in_specs, out_specs=out_specs, check_vma=False)
```

profile of v0, /device:TPU:0, one launch (start us, length us, event | category | flops | bytes accessed | tf_op | source)
XLA Modules:
  0.0 136.5 jit_solution(16700542760090385622)
XLA Ops:
  7.4 2.0 %copy.47 = f32[2,4,2,128,64]{3,4,2,0,1:T(8,128)} copy(f32[2,4,2,128,64]{3,4,2,1,0:T(8,128)} %param.9) | data formatting | bytes 1048576 | tf_op args[2]
  9.3 6.3 %all-to-all-start = ((f32[2,4,2,128,64]{3,4,2,0,1:T(8,128)}), f32[2,4,2,128,64]{3,4,2,0,1:T(8,128)S(1)}, u32[]{:S(2)}, u32[]{:S(2)}) async-start(f32[2,4,2,128,64]{3,4,2,0,1:T(8,128)} %copy.47), calls=%async_computation | async-start | bytes 1048576 | tf_op jit(solution)/shard_map/all_to_all | solution.py:63
  15.7 0.7 fusion.31
  24.0 4.0 %fusion.27 = (f32[1,3,128,256]{3,2,1,0:T(8,128)}, f32[1,3,128,256]{3,2,1,0:T(8,128)}, f32[1,3,128,256]{3,2,1,0:T(8,128)}, f32[1,3,128,256]{3,2,1,0:T(8,128)S(1)}...) fusion(f32[2,3,1,3,128,256]{5,4,3,2,1,0:T(8,128)} %param.8, ...), kind=kLoop, calls=%fused_computation.75 | loop fusion | flops 2752512 | bytes 7868436 | tf_op jit(solution)/shard_map/neg | solution.py:42
  28.0 2.2 %all-to-all-done = f32[2,4,2,128,64]{3,4,2,0,1:T(8,128)S(1)} async-done(((f32[2,4,2,128,64]{3,4,2,0,1:T(8,128)}), f32[2,4,2,128,64]{3,4,2,0,1:T(8,128)S(1)}, u32[]{:S(2)}, u32[]{:S(2)}) %all-to-all-start) | async-done | bytes 524320 | tf_op jit(solution)/shard_map/all_to_all | solution.py:63
  30.2 1.0 copy.49
  31.4 1.6 %maximum_maximum_fusion = f32[2,3,128,512]{3,2,1,0:T(8,128)S(1)} fusion(f32[1,3,128,256]{3,2,1,0:T(8,128)} %get-tuple-element.5, f32[1,3,128,256]{3,2,1,0:T(8,128)} %get-tuple-element.13, f32[1,3,128,256]{3,2,1,0:T(8,128)} %get-tuple-element.6), kind=kLoop, calls=%fused_computation.12 | loop fusion | flops 1179648 | bytes 2752512 | tf_op jit(solution)/shard_map/concatenate | solution.py:41
  33.6 10.6 %fusion.8 = f32[256,2048]{0,1:T(8,128)S(1)} fusion(f32[768,256]{1,0:T(8,128)S(1)} %bitcast.149, f32[768,512]{1,0:T(8,128)S(1)} %bitcast.158, f32[768,512]{1,0:T(8,128)S(1)} %bitcast.157, f32[768,512]{1,0:T(8,128)S(1)} %bitcast.156, f32[768,512]{1,0:T(8,128)S(1)} %bitcast.155), kind=kOutput, calls=%fused_computation.8 | convolution fusion | flops 4836556800 | bytes 9175040 | tf_op jit(solution)/shard_map/dot_general | solution.py:48
  44.2 1.8 %copy.78 = f32[256,2048]{1,0:T(8,128)} copy(f32[256,2048]{0,1:T(8,128)S(1)} %fusion.8) | data formatting | bytes 4194304
  46.1 2.9 %copy.50 = f32[2,1,4,128,256]{4,2,3,1,0:T(4,128)} copy(f32[2,1,4,128,256]{4,3,1,0,2:T(8,128)} %all-gather.4.cloned.1.call-done) | data formatting | bytes 2097152 | tf_op jit(solution)/shard_map/all_gather | solution.py:64
  49.0 0.2 all-gather.8.cloned.1.call-start
  49.3 44.4 %reduce-scatter.4.cloned.1.call-done = f32[64,2048]{1,0:T(8,128)} async-done(((f32[256,2048]{1,0:T(8,128)}), f32[64,2048]{1,0:T(8,128)}) %reduce-scatter.4.cloned.1.call-update) | async-done | bytes 524304 | tf_op jit(solution)/shard_map/reduce_scatter | solution.py:55
  93.8 4.1 %fusion.13 = f32[4,2,256,256]{3,0,2,1:T(4,128)S(1)} fusion(f32[2,1,4,256,256]{4,2,3,1,0:T(4,128)} %all-gather.6.cloned.1.call-done, f32[4,2,4,1]{2,1,0,3:T(2,128)S(1)} %get-tuple-element.27), kind=kOutput, calls=%fused_computation.22 | convolution fusion | flops 25165824 | bytes 3145856 | tf_op jit(solution)/shard_map/oab,tbls->otals/dot_general | solution.py:66
  97.9 4.5 %convolution_subtract_fusion = f32[4,2,256,256]{3,0,2,1:T(4,128)} fusion(f32[4,2,256,256]{3,0,2,1:T(4,128)S(1)} %fusion.13, f32[2,1,4,256,256]{4,2,3,1,0:T(4,128)S(1)} %copy-done.3, f32[4,2,4,1]{2,1,0,3:T(2,128)S(1)} %get-tuple-element.26), kind=kOutput, calls=%fused_computation.11 | convolution fusion | flops 25690112 | bytes 5246976 | tf_op jit(solution)/shard_map/oab,tbls->otals/dot_general | solution.py:66
  102.4 1.9 %copy.56 = f32[4,2,256,256]{2,3,1,0:T(8,128)S(1)} copy(f32[4,2,256,256]{3,0,2,1:T(4,128)} %convolution_subtract_fusion) | data formatting | bytes 4194304 | tf_op jit(solution)/shard_map/sub | solution.py:66
  104.3 4.1 %fusion.14 = f32[4,2,256,256]{3,0,2,1:T(4,128)S(1)} fusion(f32[2,1,4,256,256]{4,2,3,1,0:T(4,128)} %all-gather.6.cloned.1.call-done, f32[4,2,4,1]{2,1,0,3:T(2,128)S(1)} %get-tuple-element.27), kind=kOutput, calls=%fused_computation.23 | convolution fusion | flops 25165824 | bytes 3145856 | tf_op jit(solution)/shard_map/oab,tbls->otals/dot_general | solution.py:69
  108.5 4.5 %convolution_add_fusion = f32[4,2,256,256]{3,0,2,1:T(4,128)} fusion(f32[4,2,256,256]{3,0,2,1:T(4,128)S(1)} %fusion.14, f32[2,1,4,256,256]{4,2,3,1,0:T(4,128)S(1)} %copy-done.4, f32[4,2,4,1]{2,1,0,3:T(2,128)S(1)} %get-tuple-element.26), kind=kOutput, calls=%fused_computation.10 | convolution fusion | flops 25690112 | bytes 5246976 | tf_op jit(solution)/shard_map/oab,tbls->otals/dot_general | solution.py:69
  112.9 2.9 %copy.60 = f32[4,2,256,256]{2,3,1,0:T(8,128)} copy(f32[4,2,256,256]{3,0,2,1:T(4,128)} %convolution_add_fusion) | data formatting | bytes 4194304 | tf_op jit(solution)/shard_map/add | solution.py:69
  115.8 2.5 %copy.54 = f32[128,2048]{0,1:T(8,128)} copy(f32[128,2048]{1,0:T(8,128)} %all-gather.8.cloned.1.call-done) | data formatting | bytes 2097152 | tf_op jit(solution)/shard_map/all_gather | solution.py:56
  118.4 3.1 %fusion.16 = f32[4,2,256,128]{3,2,1,0:T(8,128)S(1)} fusion(f32[4,2,256,256]{2,3,1,0:T(8,128)S(1)} %copy.56, f32[128,1,4,2,256]{0,4,3,2,1:T(8,128)} %bitcast.150), kind=kOutput, calls=%fused_computation.27 | convolution fusion | flops 805306368 | bytes 3670016 | tf_op jit(solution)/shard_map/ktol,otals->otaks/dot_general | solution.py:75
  121.5 1.9 %fusion.15 = f32[4,2,256,128]{3,2,1,0:T(8,128)S(1)} fusion(f32[4,2,256,256]{2,3,1,0:T(8,128)S(1)} %copy-done.1, f32[128,1,4,2,256]{0,4,3,2,1:T(8,128)S(1)} %bitcast.151), kind=kOutput, calls=%fused_computation.26 | convolution fusion | flops 805306368 | bytes 3670016 | tf_op jit(solution)/shard_map/ktol,otals->otaks/dot_general | solution.py:78
  123.5 2.0 %fusion.12 = f32[1,4,1,2,128,256]{4,5,3,1,2,0:T(8,128)S(1)} fusion(f32[4,2,256,128]{3,2,1,0:T(8,128)S(1)} %fusion.16, f32[4,2,256,256]{2,3,1,0:T(8,128)S(1)} %copy-done.1, f32[128,1,4,2,256]{0,4,3,2,1:T(8,128)S(1)} %bitcast.152), kind=kOutput, calls=%fused_computation.19 | convolution fusion | flops 805568512 | bytes 4718592 | tf_op jit(solution)/shard_map/ktol,otals->otaks/dot_general | solution.py:75
  125.4 2.0 %fusion.11 = f32[1,4,1,2,128,256]{4,5,3,1,2,0:T(8,128)S(1)} fusion(f32[4,2,256,128]{3,2,1,0:T(8,128)S(1)} %fusion.15, f32[4,2,256,256]{2,3,1,0:T(8,128)S(1)} %copy.56, f32[128,1,4,2,256]{0,4,3,2,1:T(8,128)S(1)} %bitcast.153), kind=kOutput, calls=%fused_computation.17 | convolution fusion | flops 805568512 | bytes 4718592 | tf_op jit(solution)/shard_map/ktol,otals->otaks/dot_general | solution.py:78
  127.6 1.8 %copy.63 = f32[2,4,1,2,128,256]{5,4,3,2,1,0:T(8,128)} copy(f32[2,4,1,2,128,256]{4,5,3,1,2,0:T(8,128)S(1)} %pad_maximum_fusion) | data formatting | bytes 4194304 | tf_op jit(solution)/shard_map/stack | solution.py:81
  (50 shorter events, 1.1 us)
Async XLA Ops:
  7.4 26.2 %copy-start = (f32[2,1,3,128,256]{4,3,2,1,0:T(8,128)S(1)}, f32[2,1,3,128,256]{4,3,2,1,0:T(8,128)}, u32[]{:S(2)}) copy-start(f32[2,1,3,128,256]{4,3,2,1,0:T(8,128)} %param.7) | copy-start | bytes 2359300
  7.4 8.3 %copy-start.11 = (s32[4]{0:T(128)S(1)}, s32[4]{0:T(128)}, u32[]{:S(2)}) copy-start(s32[4]{0:T(128)} %param.12) | copy-start | bytes 52
  7.4 16.5 %copy-start.13 = (s32[4]{0:T(128)S(1)}, s32[4]{0:T(128)}, u32[]{:S(2)}) copy-start(s32[4]{0:T(128)} %param.13) | copy-start | bytes 52
  9.3 20.8 %all-to-all-start = ((f32[2,4,2,128,64]{3,4,2,0,1:T(8,128)}), f32[2,4,2,128,64]{3,4,2,0,1:T(8,128)S(1)}, u32[]{:S(2)}, u32[]{:S(2)}) async-start(f32[2,4,2,128,64]{3,4,2,0,1:T(8,128)} %copy.47), calls=%async_computation | async-start | bytes 1048576 | tf_op jit(solution)/shard_map/all_to_all | solution.py:63
  15.7 30.4 %all-gather.4.cloned.1.call-start = ((), (), s32[]{:S(2)}) async-start(), calls=%async_computation.2 | async-start | bytes 1572864 | tf_op jit(solution)/shard_map/all_gather | solution.py:64
  30.2 2.8 %copy-start.7 = (f32[1,3,128,256]{3,2,1,0:T(8,128)S(1)}, f32[1,3,128,256]{3,2,1,0:T(8,128)}, u32[]{:S(2)}) copy-start(f32[1,3,128,256]{3,2,1,0:T(8,128)} %get-tuple-element.23) | copy-start | bytes 1179652
  31.3 1.8 %copy-start.8 = (f32[1,3,128,256]{3,2,1,0:T(8,128)S(1)}, f32[1,3,128,256]{3,2,1,0:T(8,128)}, u32[]{:S(2)}) copy-start(f32[1,3,128,256]{3,2,1,0:T(8,128)} %get-tuple-element.24) | copy-start | bytes 1179652
  31.3 62.4 %reduce-scatter.4.cloned.1.call-start = ((), (), s32[]{:S(2)}) async-start(), calls=%async_computation.5 | async-start | bytes 2621440 | tf_op jit(solution)/shard_map/reduce_scatter | solution.py:55
  31.3 1.7 %copy-start.9 = (f32[1,3,128,256]{3,2,1,0:T(8,128)S(1)}, f32[1,3,128,256]{3,2,1,0:T(8,128)}, u32[]{:S(2)}) copy-start(f32[1,3,128,256]{3,2,1,0:T(8,128)} %get-tuple-element.25) | copy-start | bytes 1179652
  31.3 1.9 %copy-start.5 = (f32[1,3,128,256]{3,2,1,0:T(8,128)S(1)}, f32[1,3,128,256]{3,2,1,0:T(8,128)}, u32[]{:S(2)}) copy-start(f32[1,3,128,256]{3,2,1,0:T(8,128)} %get-tuple-element.21) | copy-start | bytes 1179652
  31.3 1.9 %copy-start.6 = (f32[1,3,128,256]{3,2,1,0:T(8,128)S(1)}, f32[1,3,128,256]{3,2,1,0:T(8,128)}, u32[]{:S(2)}) copy-start(f32[1,3,128,256]{3,2,1,0:T(8,128)} %get-tuple-element.22) | copy-start | bytes 1179652
  46.0 3.2 %copy-start.10 = (s32[4,4,4]{2,1,0:T(4,128)S(1)}, s32[4,4,4]{2,1,0:T(4,128)}, u32[]{:S(2)}) copy-start(s32[4,4,4]{2,1,0:T(4,128)} %param.11) | copy-start | bytes 772
  46.0 3.3 %copy-start.12 = (f32[2,4,4,4]{3,2,1,0:T(4,128)S(1)}, f32[2,4,4,4]{3,2,1,0:T(4,128)}, u32[]{:S(2)}) copy-start(f32[2,4,4,4]{3,2,1,0:T(4,128)} %param.10) | copy-start | bytes 1540
  46.0 47.7 %all-gather.6.cloned.1.call-start = ((), (), s32[]{:S(2)}) async-start(), calls=%async_computation.3 | async-start | bytes 3145728 | tf_op jit(solution)/shard_map/all_gather | solution.py:65
  49.0 66.9 %all-gather.8.cloned.1.call-start = ((), (), s32[]{:S(2)}) async-start(), calls=%async_computation.4 | async-start | bytes 1572864 | tf_op jit(solution)/shard_map/all_gather | solution.py:56
  93.7 4.1 %copy-start.3 = (f32[2,1,4,256,256]{4,2,3,1,0:T(4,128)S(1)}, f32[2,1,4,256,256]{4,2,3,1,0:T(4,128)}, u32[]{:S(2)}) copy-start(f32[2,1,4,256,256]{4,2,3,1,0:T(4,128)} %all-gather.6.cloned.1.call-done) | copy-start | bytes 6291460
  104.3 4.1 %copy-start.4 = (f32[2,1,4,256,256]{4,2,3,1,0:T(4,128)S(1)}, f32[2,1,4,256,256]{4,2,3,1,0:T(4,128)}, u32[]{:S(2)}) copy-start(f32[2,1,4,256,256]{4,2,3,1,0:T(4,128)} %all-gather.6.cloned.1.call-done) | copy-start | bytes 6291460
  118.4 3.1 %copy-start.1 = (f32[4,2,256,256]{2,3,1,0:T(8,128)S(1)}, f32[4,2,256,256]{2,3,1,0:T(8,128)}, u32[]{:S(2)}) copy-start(f32[4,2,256,256]{2,3,1,0:T(8,128)} %copy.60) | copy-start | bytes 6291460
  118.4 3.1 %copy-start.2 = (f32[128,2048]{0,1:T(8,128)S(1)}, f32[128,2048]{0,1:T(8,128)}, u32[]{:S(2)}) copy-start(f32[128,2048]{0,1:T(8,128)} %copy.54) | copy-start | bytes 3145732
Sparse Core Ops, SparseCore 0:
  31.4 8.3 all-gather.3
  49.1 32.7 all-gather.5
  93.8 8.9 all-gather.7
Sparse Core Ops, SparseCore 1:
  46.1 47.5 reduce-scatter.3
where the time goes:
time: 137 us
  waiting for transfers between devices  46.6 us (34%)
  matrix products  36.8 us (27%)
  between operations  22.4 us (16%)
  local copies, waits for them, and re-layouts  17.6 us (13%)
  starting transfers between devices  6.66 us (5%)
  other arithmetic  6.41 us (5%)
    reduce_scatter x1, waiting for transfers between devices, local(): lax.psum_scatter(pieces, ('space', 'spin'), scatter_dimension=0, tiled=True)  44.4 us
    dot_general x1, matrix products, local(): lax.dot_general(left_rows, rights[tslice], (((0,), (0,)), ((), ())), prec...  10.6 us
    all_to_all x1, starting transfers between devices, local(): lax.all_to_all(perambulators, 'tm', split_axis=1, concat_axis=4, tiled=True)  6.35 us
    dot_general x1, matrix products, local(): jnp.einsum('oab,tbls->otals', spin_rows[1], piece[1], precision=highest)  4.46 us
    dot_general x1, matrix products, local(): jnp.einsum('oab,tbls->otals', spin_rows[1], piece[0], precision=highest)  4.46 us
    dot_general x1, matrix products, local(): jnp.einsum('oab,tbls->otals', spin_rows[0], piece[0], precision=highest)  4.13 us
    dot_general x1, matrix products, local(): jnp.einsum('oab,tbls->otals', spin_rows[0], piece[1], precision=highest)  4.13 us
    neg x1, other arithmetic, local(): -real_w  3.97 us
  transfers between devices with their start and end apart: 5, of which 2 were waited for; matrix products, arithmetic and copies ran while one was open for 32% of the time, Pallas kernels for 0%

commit v1 on v0

v1 whole, which is shorter than its diff:
```python
import functools
import math

import numpy as np

import jax
import jax.numpy as jnp
from jax import lax
from jax.experimental import pallas as pl
from jax.experimental.pallas import tpu as pltpu
from jax.sharding import PartitionSpec as P

f32 = jnp.float32
bf16 = jnp.bfloat16
VMEM = pl.BlockSpec(memory_space=pltpu.VMEM)
SMEM = pl.BlockSpec(memory_space=pltpu.SMEM)


def cut(value):
    high = value.astype(bf16)
    return high, (value - high.astype(f32)).astype(bf16)


def place(bits):
    return jnp.stack([lax.axis_index(axis) for axis in bits]).astype(jnp.int32)


def partner(value, axis, distance):
    size = lax.axis_size(axis)
    return lax.ppermute(value, axis, [(i, i ^ distance) for i in range(size)])


def pack_body(where, peram, *outs):
    for distance, out in enumerate(outs):
        for part in range(peram.shape[0]):
            out[part] = peram[part, where[1] ^ distance]


def pack(where, peram):
    parts, times = peram.shape[:2]
    shape = jax.ShapeDtypeStruct((parts,) + peram.shape[2:], f32)
    return pl.pallas_call(
        pack_body,
        out_shape=[shape] * times,
        in_specs=[SMEM, VMEM],
        out_specs=[VMEM] * times,
        name="pack",
        cost_estimate=pl.CostEstimate(flops=0, bytes_accessed=peram.size * 8, transcendentals=0),
        compiler_params=pltpu.CompilerParams(vmem_limit_bytes=8 << 20),
    )(where, peram)


def sums_body(chips, cores, where, vectors, moved, own, keep, send, left_high, left_low):
    colours, sites, width = vectors.shape[2:]
    depth = colours * sites

    @pl.when(pl.program_id(0) == 0)
    def _():
        for colour in range(colours):
            at = colour * sites
            real = vectors[0, 0, colour].T
            imag = vectors[1, 0, colour].T
            for row, first, value in (
                (0, 0, real),
                (0, depth, imag),
                (width, 0, -imag),
                (width, depth, real),
            ):
                high, low = cut(value)
                left_high[row : row + width, first + at : first + at + sites] = high
                left_low[row : row + width, first + at : first + at + sites] = low

    right = jnp.concatenate([moved[part, 0, 0, colour] for part in range(2) for colour in range(colours)])
    high, low = cut(right)
    rows = width // (chips * cores)

    def product(start, count):
        a_high = left_high[pl.ds(start, count), :]
        a_low = left_low[pl.ds(start, count), :]
        dot = functools.partial(jnp.dot, preferred_element_type=f32)
        return dot(a_high, high) + dot(a_high, low) + dot(a_low, high)

    for part in range(2):
        base = part * width
        first = pl.multiple_of(base + where[2] * cores * rows, cores * rows)
        own[0, part] = product(first, cores * rows)
        for away in range(1, chips):
            chip = where[2] ^ away
            for core, out in ((0, keep), (1, send)):
                start = pl.multiple_of(base + (chip * cores + (where[3] ^ core)) * rows, rows)
                out[0, away - 1, part] = product(start, rows)


def sums(where, vectors, displaced, chips, cores):
    colours, sites, width = vectors.shape[2:]
    kinds = displaced.shape[1]
    rows = width // (chips * cores)
    depth = 2 * colours * sites
    own = jax.ShapeDtypeStruct((kinds, 2, rows * cores, width), f32)
    other = jax.ShapeDtypeStruct((kinds, chips - 1, 2, rows, width), f32)
    return pl.pallas_call(
        functools.partial(sums_body, chips, cores),
        out_shape=[own, other, other],
        grid=(kinds,),
        in_specs=[
            SMEM,
            pl.BlockSpec(vectors.shape, lambda i: (0,) * 5, pipeline_mode=pl.Buffered(1)),
            pl.BlockSpec((2, 1) + displaced.shape[2:], lambda i: (0, i, 0, 0, 0, 0)),
        ],
        out_specs=[
            pl.BlockSpec((1,) + own.shape[1:], lambda i: (i, 0, 0, 0)),
            pl.BlockSpec((1,) + other.shape[1:], lambda i: (i, 0, 0, 0, 0)),
            pl.BlockSpec((1,) + other.shape[1:], lambda i: (i, 0, 0, 0, 0)),
        ],
        scratch_shapes=[pltpu.VMEM((2 * width, depth), bf16)] * 2,
        name="sums",
        cost_estimate=pl.CostEstimate(
            flops=12 * width * depth * width * kinds,
            bytes_accessed=4 * (vectors.size + displaced.size) + 4 * kinds * 4 * width * width,
            transcendentals=0,
        ),
        compiler_params=pltpu.CompilerParams(vmem_limit_bytes=24 << 20, dimension_semantics=("arbitrary",)),
    )(where, vectors, displaced)


def phase(turns, chips, table):
    value = f32(table[0])
    for step in range(1, chips):
        value = jnp.where(turns == step, f32(table[step]), value)
    return value


def products_body(
    chips, cores, half, tables, where, gamma, pattern, directions, momenta, mine, theirs, *rest
):
    away_count = chips - 1
    far = rest[:away_count]
    far_other = rest[away_count : 2 * away_count]
    rest = rest[2 * away_count :]
    blocks = rest[: half * chips * cores]
    rest = rest[half * chips * cores :]
    if len(rest) == 5:
        rest = rest[1:]
    out, spread, e_high, e_low = rest
    operator = pl.program_id(0)
    row_count, width = mine.shape[2:]
    per_core, cols, depth_rows = blocks[0].shape[1:]

    @pl.when(operator == 0)
    def _():
        for step in range(half):
            at = pl.multiple_of(((where[1] ^ step) & (half - 1)) * cols, cols)
            for away in range(chips):
                for core in range(cores):
                    block = blocks[(step * chips + away) * cores + core]
                    for part in range(2):
                        for spin in range(per_core):
                            spread[
                                part,
                                core * per_core + spin,
                                pl.ds(at, cols),
                                away * depth_rows : (away + 1) * depth_rows,
                            ] = block[part, spin]

    kind = directions[operator]
    real = jnp.zeros((row_count, width), f32)
    imag = jnp.zeros((row_count, width), f32)
    for away in range(chips):
        turns = lax.rem(momenta[operator] * (where[2] ^ away), chips)
        cosine = phase(turns, chips, tables[0])
        sine = phase(turns, chips, tables[1])
        if away == 0:
            pair = [mine[kind, part] + theirs[kind, part] for part in range(2)]
        else:
            here = [far[away - 1][kind, part] for part in range(2)]
            there = [far_other[away - 1][kind, part] for part in range(2)]
            first = where[3] == 0
            pair = [
                jnp.concatenate([jnp.where(first, a, b), jnp.where(first, b, a)])
                for a, b in zip(here, there)
            ]
        real = real + cosine * pair[0] + sine * pair[1]
        imag = imag + cosine * pair[1] - sine * pair[0]
    lane = lax.broadcasted_iota(jnp.int32, (row_count, width), 1)
    bit = 1
    while bit < chips:
        reach = bit * depth_rows
        turned = []
        for value in (real, imag):
            up = pltpu.roll(value, width - reach, 1)
            down = up if 2 * reach == width else pltpu.roll(value, reach, 1)
            swapped = jnp.where((lane & reach) == 0, up, down)
            turned.append(jnp.where((where[2] & bit) != 0, swapped, value))
        real, imag = turned
        bit *= 2
    for value, sign, spots in (
        (real, 1.0, ((0, 0), (row_count, width))),
        (imag, 1.0, ((row_count, 0),)),
        (imag, -1.0, ((0, width),)),
    ):
        high, low = cut(sign * value)
        for row, col in spots:
            e_high[row : row + row_count, col : col + width] = high
            e_low[row : row + row_count, col : col + width] = low

    sinks = out.shape[3]
    mixed = []
    for sink in range(sinks):
        row = where[3] * sinks + sink
        mixed_real = None
        mixed_imag = None
        for core in range(cores):
            for spin in range(per_core):
                source = (where[3] ^ core) * per_core + spin
                on = pattern[operator, row, source].astype(f32)
                g_real = gamma[0, operator, row, source] * on
                g_imag = gamma[1, operator, row, source] * on
                p_real = spread[0, core * per_core + spin]
                p_imag = spread[1, core * per_core + spin]
                one = g_real * p_real - g_imag * p_imag
                two = g_real * p_imag + g_imag * p_real
                mixed_real = one if mixed_real is None else mixed_real + one
                mixed_imag = two if mixed_imag is None else mixed_imag + two
        mixed.append(jnp.concatenate([mixed_real, mixed_imag], axis=1))
    high, low = cut(jnp.concatenate(mixed))

    def dot(left, right):
        return lax.dot_general(left, right, (((1,), (1,)), ((), ())), preferred_element_type=f32)

    result = dot(e_high[...], high) + dot(e_high[...], low) + dot(e_low[...], high)
    lanes = out.shape[5]
    for sink in range(sinks):
        out[0, 0, 0, sink] = result[:row_count, sink * lanes : (sink + 1) * lanes]
        out[1, 0, 0, sink] = result[row_count:, sink * lanes : (sink + 1) * lanes]


def products(side, where, scalars, mine, theirs, far, far_other, blocks, shape, chips, cores, previous):
    half = len(blocks) // (chips * cores)
    width = mine.shape[-1]
    spins = scalars[0].shape[2]
    lanes = shape[-1] // 2
    rows = mine.shape[2]
    times = 2 * half
    tables = [
        [float(v) for v in fn(np.arange(chips, dtype=np.float32) * np.float32(2.0 * math.pi / chips))]
        for fn in (np.cos, np.sin)
    ]
    operands = [where, *scalars, mine, theirs, *far, *far_other, *blocks]
    specs = [SMEM] * 5 + [VMEM] * (len(operands) - 5)
    aliases = {}
    if previous is not None:
        aliases = {len(operands): 0}
        operands.append(previous)
        specs.append(pl.BlockSpec(memory_space=pl.ANY))
    specs = [
        pl.BlockSpec(memory_space=s.memory_space) if s is not SMEM else s for s in specs
    ]
    return pl.pallas_call(
        functools.partial(products_body, chips, cores, half, tables),
        out_shape=jax.ShapeDtypeStruct(shape, f32),
        grid_spec=pltpu.PrefetchScalarGridSpec(
            num_scalar_prefetch=1,
            grid=(shape[1],),
            in_specs=specs[1:],
            out_specs=pl.BlockSpec(
                (2, 1, 1) + shape[3:5] + (lanes,),
                lambda o, where: (0, o, 0, 0, 0, (where[1] // half) ^ side),
            ),
            scratch_shapes=[
                pltpu.VMEM((2, spins, lanes, width), f32),
                pltpu.VMEM((2 * rows, 2 * width), bf16),
                pltpu.VMEM((2 * rows, 2 * width), bf16),
            ],
        ),
        input_output_aliases=aliases,
        name=f"products_{side}",
        cost_estimate=pl.CostEstimate(
            flops=3 * 2 * shape[1] * shape[3] * 2 * rows * 2 * width * lanes,
            bytes_accessed=4 * math.prod(shape) // 2,
            transcendentals=0,
        ),
        compiler_params=pltpu.CompilerParams(vmem_limit_bytes=24 << 20, dimension_semantics=("arbitrary",)),
    )(*operands)


def local(eigenvectors, displaced, perambulators, gamma_values, spin_pattern, directions, momenta):
    width = eigenvectors.shape[4]
    operators = gamma_values.shape[1]
    spins = gamma_values.shape[2]
    times = lax.axis_size("tm")
    chips = lax.axis_size("space")
    cores = lax.axis_size("spin")
    where = place(("parts", "tm", "space", "spin"))
    half = times // 2

    mine_blocks = pack(where, jnp.swapaxes(perambulators, 3, 4))
    near = [mine_blocks[0]] + [partner(mine_blocks[d], "tm", d) for d in range(1, times)]
    own, keep, send = sums(where, eigenvectors, displaced, chips, cores)
    far_sum = keep + partner(send, "spin", 1)
    theirs = partner(own, "spin", 1)
    far = [partner(far_sum[:, away - 1], "space", away) for away in range(1, chips)]
    far_other = [partner(value, "spin", 1) for value in far]
    gathered = []
    for d in range(times):
        chip_blocks = [near[d]] + [partner(near[d], "space", away) for away in range(1, chips)]
        gathered.append([(block, partner(block, "spin", 1)) for block in chip_blocks])

    scalars = [gamma_values, spin_pattern, directions, momenta]
    shape = (2, operators, eigenvectors.shape[1], spins // cores, width // chips, perambulators.shape[4] * times)
    result = None
    for side in range(2):
        blocks = [
            block
            for d in range(side * half, (side + 1) * half)
            for pair in gathered[d]
            for block in pair
        ]
        result = products(side, where, scalars, own, theirs, far, far_other, blocks, shape, chips, cores, result)
    return result


def solution(mesh):
    in_specs = (
        P(None, ("parts", "tm"), None, ("space", "spin"), None),
        P(None, None, ("parts", "tm"), None, ("space", "spin"), None),
        P(None, "parts", "spin", "space", "tm"),
        P(),
        P(),
        P(),
        P(),
    )
    out_specs = P(None, None, ("parts", "tm"), "spin", "space", None)
    return jax.shard_map(local, mesh=mesh, in_specs=in_specs, out_specs=out_specs, check_vma=False)
```

time: 137 us -> 52.2 us (0.38)
  matrix products: 36.8 us -> 0 us
  waiting for transfers between devices: 46.6 us -> 19.5 us
  between operations: 22.4 us -> 0.1 us
  Pallas kernels: 0 us -> 16 us
  local copies, waits for them, and re-layouts: 17.6 us -> 2.82 us
  starting transfers between devices: 6.66 us -> 13.4 us
  other arithmetic: 6.41 us -> 0.13 us
    reduce_scatter x1 -> x0, waiting for transfers between devices: 44.4 us -> none  [local(): lax.psum_scatter(pieces, ('space', 'spin'), scatter_dimension=0, tiled=True)]
    dot_general x9 -> x0, matrix products: 36.8 us -> none  [the longest x1 10.6 us: local(): lax.dot_general(left_rows, rights[tslice], (((0,), (0,)), ((), ())), prec...]
    ppermute x0 -> x19, waiting for transfers between devices: none -> 19.5 us  [partner(): return lax.ppermute(value, axis, [(i, i ^ distance) for i in range(size)])]
    pallas_call x0 -> x4, Pallas kernels: none -> 16 us  [the longest x2 10.7 us: products(): pl.pallas_call(functools.partial(products_body, chips, cores, half, table...]
    ppermute x0 -> x19, starting transfers between devices: none -> 13.4 us  [partner(): return lax.ppermute(value, axis, [(i, i ^ distance) for i in range(size)])]
    all_to_all x1 -> x0, starting transfers between devices: 6.35 us -> none  [local(): lax.all_to_all(perambulators, 'tm', split_axis=1, concat_axis=4, tiled=True)]
    all_gather x2 -> x0, local copies, waits for them, and re-layouts: 5.4 us -> none  [the longest x1 2.87 us: local(): arrived = lax.all_gather(arrived, 'spin', axis=2, tiled=True)]
    neg x1 -> x0, other arithmetic: 3.97 us -> none  [local(): -real_w]
  transfers between devices with their start and end apart: 5 -> 19, of which waited for: 2 -> 7; matrix products, arithmetic and copies ran while one was open for 32% -> 0% of each run, Pallas kernels for 0% -> 11%
where the time goes in v1:
time: 52.2 us; the launch traced here: 52 us
  waiting for transfers between devices  19.5 us (37%)
  Pallas kernels  16 us (31%)
  starting transfers between devices  13.4 us (26%)
  local copies, waits for them, and re-layouts  2.82 us (5%)
    ppermute x19, waiting for transfers between devices, partner(): return lax.ppermute(value, axis, [(i, i ^ distance) for i in range(size)])  19.5 us
    ppermute x19, starting transfers between devices, partner(): return lax.ppermute(value, axis, [(i, i ^ distance) for i in range(size)])  13.4 us
    pallas_call x2, Pallas kernels, products(): pl.pallas_call(functools.partial(products_body, chips, cores, half, table...  10.7 us
    pallas_call x1, Pallas kernels, sums(): pl.pallas_call(functools.partial(sums_body, chips, cores), out_shape=[own...  4.72 us
    unnamed x14, local copies, waits for them, and re-layouts  2.82 us
  transfers between devices with their start and end apart: 19, of which 7 were waited for; matrix products, arithmetic and copies ran while one was open for 0% of the time, Pallas kernels for 11%

profile of v1, /device:TPU:0, one launch (start us, length us, event | category | flops | bytes accessed | tf_op | source)
XLA Modules:
  0.0 52.0 jit_solution(6574252911166218007)
XLA Ops:
  0.1 1.7 %copy-done.5 = f32[2,3,1,3,128,256]{5,4,3,2,1,0:T(8,128)S(1)} copy-done((f32[2,3,1,3,128,256]{5,4,3,2,1,0:T(8,128)S(1)}, f32[2,3,1,3,128,256]{5,4,3,2,1,0:T(8,128)}, u32[]{:S(2)}) %copy-start.5) | copy-done | bytes 2359320
  1.7 1.1 %copy-done.6 = f32[2,1,3,128,256]{4,3,2,1,0:T(8,128)S(1)} copy-done((f32[2,1,3,128,256]{4,3,2,1,0:T(8,128)S(1)}, f32[2,1,3,128,256]{4,3,2,1,0:T(8,128)}, u32[]{:S(2)}) %copy-start.6) | copy-done | bytes 786456
  2.9 4.7 %sums.1 = (f32[3,2,128,256]{3,2,1,0:T(8,128)S(1)}, f32[3,1,2,64,256]{4,3,2,1,0:T(8,128)S(1)}, f32[3,1,2,64,256]{4,3,2,1,0:T(8,128)S(1)}) custom-call(s32[4]{0:T(128)S(1)} %pad_add_fusion.where, f32[2,1,3,128,256]{4,3,2,1,0:T(8,128)S(1)} %copy-done.6, f32[2,3,1,3,128,256]{5,4,3,2,1,0:T(8,128)S(1)} %copy-done.5), custom_call_target="tpu_custom_call" | custom-call | flops 1811939328 | bytes 6291456 | tf_op jit(solution)/shard_map/sums/pallas_call | solution.py:101
  7.6 0.6 %collective-permute-start.1 = (f32[3,1,2,64,256]{4,3,2,0,1:T(8,128)S(1)}, f32[3,1,2,64,256]{4,3,2,0,1:T(8,128)S(1)}, u32[]{:S(2)}, u32[]{:S(2)}) collective-permute-start(f32[3,1,2,64,256]{4,3,2,0,1:T(8,128)S(1)} %bitcast.13), channel_id=1, source_target_pairs={{0,1},{1,0},{2,3},{3,2},{4,5},{5,4},{6,7},{7,6},{8,9},{9,8},{10,11... | collective-permute-start | bytes 1179656 | tf_op jit(solution)/shard_map/ppermute | solution.py:30
  8.3 1.3 %collective-permute-done.1 = f32[3,1,2,64,256]{4,3,2,0,1:T(8,128)S(1)} collective-permute-done((f32[3,1,2,64,256]{4,3,2,0,1:T(8,128)S(1)}, f32[3,1,2,64,256]{4,3,2,0,1:T(8,128)S(1)}, u32[]{:S(2)}, u32[]{:S(2)}) %collective-permute-start.1) | collective-permute-done | bytes 393248 | tf_op jit(solution)/shard_map/ppermute | solution.py:30
  9.6 2.9 %collective-permute-start.2 = (f32[3,2,64,256]{3,2,1,0:T(8,128)S(1)}, f32[3,2,64,256]{3,2,1,0:T(8,128)S(1)}, u32[]{:S(2)}, u32[]{:S(2)}) collective-permute-start(f32[3,2,64,256]{3,2,1,0:T(8,128)S(1)} %fusion), channel_id=1, source_target_pairs={{0,2},{2,0},{1,3},{3,1},{4,6},{6,4},{5,7},{7,5},{8,10},{10,8},{9,1... | collective-permute-start | bytes 1179656 | tf_op jit(solution)/shard_map/ppermute | solution.py:30
  12.5 0.6 %pack.1 = (f32[2,2,64,128]{3,2,1,0:T(8,128)S(1)}, f32[2,2,64,128]{3,2,1,0:T(8,128)S(1)}, f32[2,2,64,128]{3,2,1,0:T(8,128)S(1)}, f32[2,2,64,128]{3,2,1,0:T(8,128)S(1)}) custom-call(s32[4]{0:T(128)S(1)} %pad_add_fusion.where, f32[2,4,2,64,128]{4,3,2,1,0:T(8,128)S(1)} %bitcast.12), custom_call_target="tpu_custom_call" | custom-call | bytes 1048576 | tf_op jit(solution)/shard_map/pack/pallas_call | solution.py:42
  13.1 2.6 %collective-permute-start.4 = (f32[2,2,64,128]{3,2,1,0:T(8,128)S(1)}, f32[2,2,64,128]{3,2,1,0:T(8,128)S(1)}, u32[]{:S(2)}, u32[]{:S(2)}) collective-permute-start(f32[2,2,64,128]{3,2,1,0:T(8,128)S(1)} %get-tuple-element.15), channel_id=1, source_target_pairs={{0,8},{4,12},{8,0},{12,4},{1,9},{5,13},{9,1},{13,5},{2,10},{6,14},... | collective-permute-start | bytes 393224 | tf_op jit(solution)/shard_map/ppermute | solution.py:30
  15.8 1.3 %collective-permute-start.8 = (f32[2,2,64,128]{3,2,1,0:T(8,128)S(1)}, f32[2,2,64,128]{3,2,1,0:T(8,128)S(1)}, u32[]{:S(2)}, u32[]{:S(2)}) collective-permute-start(f32[2,2,64,128]{3,2,1,0:T(8,128)S(1)} %get-tuple-element.16), channel_id=1, source_target_pairs={{0,12},{4,8},{8,4},{12,0},{1,13},{5,9},{9,5},{13,1},{2,14},{6,10},... | collective-permute-start | bytes 393224 | tf_op jit(solution)/shard_map/ppermute | solution.py:30
  17.1 0.2 collective-permute-start.15
  17.3 8.8 %collective-permute-done.4.rest_2_ = f32[2,2,64,128]{3,2,1,0:T(8,128)S(1)} collective-permute-done((f32[2,2,64,128]{3,2,1,0:T(8,128)S(1)}, f32[2,2,64,128]{3,2,1,0:T(8,128)S(1)}, u32[]{:S(2)}, u32[]{:S(2)}) %collective-permute-start.4) | collective-permute-done | bytes 131104 | tf_op jit(solution)/shard_map/ppermute | solution.py:30
  26.1 0.2 collective-permute-start.13
  26.3 0.5 collective-permute-start.3
  26.8 1.8 %collective-permute-start.6 = (f32[2,2,64,128]{3,2,1,0:T(8,128)S(1)}, f32[2,2,64,128]{3,2,1,0:T(8,128)S(1)}, u32[]{:S(2)}, u32[]{:S(2)}) collective-permute-start(f32[2,2,64,128]{3,2,1,0:T(8,128)S(1)} %collective-permute-done.4.rest_2_), channel_id=1, source_target_pairs={{0,2},{2,0},{1,3},{3,1},{4,6},{6,4},{5,7},{7,5},{8,10},{10,8},{9,1... | collective-permute-start | bytes 393224 | tf_op jit(solution)/shard_map/ppermute | solution.py:30
  28.6 3.8 %collective-permute-done.13.rest_4_ = f32[2,2,64,128]{3,2,1,0:T(8,128)S(1)} collective-permute-done((f32[2,2,64,128]{3,2,1,0:T(8,128)S(1)}, f32[2,2,64,128]{3,2,1,0:T(8,128)S(1)}, u32[]{:S(2)}, u32[]{:S(2)}) %collective-permute-start.13) | collective-permute-done | bytes 131104 | tf_op jit(solution)/shard_map/ppermute | solution.py:30
  32.5 2.0 %collective-permute-start.17 = (f32[2,2,64,128]{3,2,1,0:T(8,128)S(1)}, f32[2,2,64,128]{3,2,1,0:T(8,128)S(1)}, u32[]{:S(2)}, u32[]{:S(2)}) collective-permute-start(f32[2,2,64,128]{3,2,1,0:T(8,128)S(1)} %collective-permute-done.15.rest_6_), channel_id=1, source_target_pairs={{0,2},{2,0},{1,3},{3,1},{4,6},{6,4},{5,7},{7,5},{8,10},{10,8},{9,1... | collective-permute-start | bytes 393224 | tf_op jit(solution)/shard_map/ppermute | solution.py:30
  34.5 0.8 %collective-permute-done.6.rest_4_ = f32[2,2,64,128]{3,2,1,0:T(8,128)S(1)} collective-permute-done((f32[2,2,64,128]{3,2,1,0:T(8,128)S(1)}, f32[2,2,64,128]{3,2,1,0:T(8,128)S(1)}, u32[]{:S(2)}, u32[]{:S(2)}) %collective-permute-start.6) | collective-permute-done | bytes 131104 | tf_op jit(solution)/shard_map/ppermute | solution.py:30
  35.3 2.7 %collective-permute-done.10.rest_8_ = f32[2,2,64,128]{3,2,1,0:T(8,128)S(1)} collective-permute-done((f32[2,2,64,128]{3,2,1,0:T(8,128)S(1)}, f32[2,2,64,128]{3,2,1,0:T(8,128)S(1)}, u32[]{:S(2)}, u32[]{:S(2)}) %collective-permute-start.10) | collective-permute-done | bytes 131104 | tf_op jit(solution)/shard_map/ppermute | solution.py:30
  38.0 1.4 %collective-permute-done.17.rest_8_ = f32[2,2,64,128]{3,2,1,0:T(8,128)S(1)} collective-permute-done((f32[2,2,64,128]{3,2,1,0:T(8,128)S(1)}, f32[2,2,64,128]{3,2,1,0:T(8,128)S(1)}, u32[]{:S(2)}, u32[]{:S(2)}) %collective-permute-start.17) | collective-permute-done | bytes 131104 | tf_op jit(solution)/shard_map/ppermute | solution.py:30
  39.4 0.5 collective-permute-start.5
  40.0 0.8 %collective-permute-done.18.rest_9_ = f32[2,2,64,128]{3,2,1,0:T(8,128)S(1)} collective-permute-done((f32[2,2,64,128]{3,2,1,0:T(8,128)S(1)}, f32[2,2,64,128]{3,2,1,0:T(8,128)S(1)}, u32[]{:S(2)}, u32[]{:S(2)}) %collective-permute-start.18) | collective-permute-done | bytes 131104 | tf_op jit(solution)/shard_map/ppermute | solution.py:30
  40.9 0.4 collective-permute-start.11
  41.3 5.4 %products_0.1.rest_10_ = f32[2,4,1,2,128,256]{5,4,3,2,1,0:T(8,128)} custom-call(s32[4]{0:T(128)S(1)} %pad_add_fusion.where, f32[2,4,4,4]{3,2,1,0:T(4,128)S(1)} %copy-done.1, s32[4,4,4]{2,1,0:T(4,128)S(1)} %copy-done.2, s32[4]{0:T(128)S(1)} %copy-done.3, s32[4]{0:T(128)S(1)} %copy-done.4, f32[3,2,128,256]{3,2,1,0:T(8,128)S(1)} %get-tuple-element.12.mine, ...), custom_call_target="tpu_custom_call" | custom-call | flops 805306368 | bytes 1048576 | tf_op jit(solution)/shard_map/products_0/pallas_call | solution.py:258
  46.7 5.4 %products_1.1 = f32[2,4,1,2,128,256]{5,4,3,2,1,0:T(8,128)} custom-call(s32[4]{0:T(128)S(1)} %pad_add_fusion.where, f32[2,4,4,4]{3,2,1,0:T(4,128)S(1)} %copy-done.1, s32[4,4,4]{2,1,0:T(4,128)S(1)} %copy-done.2, s32[4]{0:T(128)S(1)} %copy-done.3, s32[4]{0:T(128)S(1)} %copy-done.4, ...), custom_call_target="tpu_custom_call", output_to_operand_aliasing={{}: (17, {})} | custom-call | flops 805306368 | bytes 1048576 | tf_op jit(solution)/shard_map/products_1/pallas_call | solution.py:258
  (34 shorter events, 0.5 us)
Async XLA Ops:
  2.9 9.7 %copy-start = (f32[2,4,2,128,64]{3,4,2,1,0:T(8,128)S(1)}, f32[2,4,2,128,64]{3,4,2,1,0:T(8,128)}, u32[]{:S(2)}) copy-start(f32[2,4,2,128,64]{3,4,2,1,0:T(8,128)} %param.9) | copy-start | bytes 1572868
  2.9 38.4 %copy-start.1 = (f32[2,4,4,4]{3,2,1,0:T(4,128)S(1)}, f32[2,4,4,4]{3,2,1,0:T(4,128)}, u32[]{:S(2)}) copy-start(f32[2,4,4,4]{3,2,1,0:T(4,128)} %gamma.3) | copy-start | bytes 1540
  2.9 38.4 %copy-start.2 = (s32[4,4,4]{2,1,0:T(4,128)S(1)}, s32[4,4,4]{2,1,0:T(4,128)}, u32[]{:S(2)}) copy-start(s32[4,4,4]{2,1,0:T(4,128)} %pattern.3) | copy-start | bytes 772
  2.9 38.4 %copy-start.3 = (s32[4]{0:T(128)S(1)}, s32[4]{0:T(128)}, u32[]{:S(2)}) copy-start(s32[4]{0:T(128)} %directions.3) | copy-start | bytes 52
  2.9 38.4 %copy-start.4 = (s32[4]{0:T(128)S(1)}, s32[4]{0:T(128)}, u32[]{:S(2)}) copy-start(s32[4]{0:T(128)} %momenta.3) | copy-start | bytes 52
  7.6 1.9 %collective-permute-start.1 = (f32[3,1,2,64,256]{4,3,2,0,1:T(8,128)S(1)}, f32[3,1,2,64,256]{4,3,2,0,1:T(8,128)S(1)}, u32[]{:S(2)}, u32[]{:S(2)}) collective-permute-start(f32[3,1,2,64,256]{4,3,2,0,1:T(8,128)S(1)} %bitcast.13), channel_id=1, source_target_pairs={{0,1},{1,0},{2,3},{3,2},{4,5},{5,4},{6,7},{7,6},{8,9},{9,8},{10,11... | collective-permute-start | bytes 1179656 | tf_op jit(solution)/shard_map/ppermute | solution.py:30
  8.2 32.7 %collective-permute-start = (f32[3,2,128,256]{3,2,1,0:T(8,128)S(1)}, f32[3,2,128,256]{3,2,1,0:T(8,128)S(1)}, u32[]{:S(2)}, u32[]{:S(2)}) collective-permute-start(f32[3,2,128,256]{3,2,1,0:T(8,128)S(1)} %get-tuple-element.12.mine), channel_id=1, source_target_pairs={{0,1},{1,0},{2,3},{3,2},{4,5},{5,4},{6,7},{7,6},{8,9},{9,8},{10,11... | collective-permute-start | bytes 2359304 | tf_op jit(solution)/shard_map/ppermute | solution.py:30
  9.6 16.7 %collective-permute-start.2 = (f32[3,2,64,256]{3,2,1,0:T(8,128)S(1)}, f32[3,2,64,256]{3,2,1,0:T(8,128)S(1)}, u32[]{:S(2)}, u32[]{:S(2)}) collective-permute-start(f32[3,2,64,256]{3,2,1,0:T(8,128)S(1)} %fusion), channel_id=1, source_target_pairs={{0,2},{2,0},{1,3},{3,1},{4,6},{6,4},{5,7},{7,5},{8,10},{10,8},{9,1... | collective-permute-start | bytes 1179656 | tf_op jit(solution)/shard_map/ppermute | solution.py:30
  13.1 13.0 %collective-permute-start.4 = (f32[2,2,64,128]{3,2,1,0:T(8,128)S(1)}, f32[2,2,64,128]{3,2,1,0:T(8,128)S(1)}, u32[]{:S(2)}, u32[]{:S(2)}) collective-permute-start(f32[2,2,64,128]{3,2,1,0:T(8,128)S(1)} %get-tuple-element.15), channel_id=1, source_target_pairs={{0,8},{4,12},{8,0},{12,4},{1,9},{5,13},{9,1},{13,5},{2,10},{6,14},... | collective-permute-start | bytes 393224 | tf_op jit(solution)/shard_map/ppermute | solution.py:30
  15.8 10.5 %collective-permute-start.8 = (f32[2,2,64,128]{3,2,1,0:T(8,128)S(1)}, f32[2,2,64,128]{3,2,1,0:T(8,128)S(1)}, u32[]{:S(2)}, u32[]{:S(2)}) collective-permute-start(f32[2,2,64,128]{3,2,1,0:T(8,128)S(1)} %get-tuple-element.16), channel_id=1, source_target_pairs={{0,12},{4,8},{8,4},{12,0},{1,13},{5,9},{9,5},{13,1},{2,14},{6,10},... | collective-permute-start | bytes 393224 | tf_op jit(solution)/shard_map/ppermute | solution.py:30
  17.1 9.7 %collective-permute-start.15 = (f32[2,2,64,128]{3,2,1,0:T(8,128)S(1)}, f32[2,2,64,128]{3,2,1,0:T(8,128)S(1)}, u32[]{:S(2)}, u32[]{:S(2)}) collective-permute-start(f32[2,2,64,128]{3,2,1,0:T(8,128)S(1)} %get-tuple-element.18), channel_id=1, source_target_pairs={{0,4},{4,0},{8,12},{12,8},{1,5},{5,1},{9,13},{13,9},{2,6},{6,2},{1... | collective-permute-start | bytes 393224 | tf_op jit(solution)/shard_map/ppermute | solution.py:30
  26.1 6.4 %collective-permute-start.13 = (f32[2,2,64,128]{3,2,1,0:T(8,128)S(1)}, f32[2,2,64,128]{3,2,1,0:T(8,128)S(1)}, u32[]{:S(2)}, u32[]{:S(2)}) collective-permute-start(f32[2,2,64,128]{3,2,1,0:T(8,128)S(1)} %get-tuple-element.17.rest_2_), channel_id=1, source_target_pairs={{0,2},{2,0},{1,3},{3,1},{4,6},{6,4},{5,7},{7,5},{8,10},{10,8},{9,1... | collective-permute-start | bytes 393224 | tf_op jit(solution)/shard_map/ppermute | solution.py:30
  26.3 6.2 %collective-permute-start.12 = (f32[2,2,64,128]{3,2,1,0:T(8,128)S(1)}, f32[2,2,64,128]{3,2,1,0:T(8,128)S(1)}, u32[]{:S(2)}, u32[]{:S(2)}) collective-permute-start(f32[2,2,64,128]{3,2,1,0:T(8,128)S(1)} %get-tuple-element.17.rest_2_), channel_id=1, source_target_pairs={{0,1},{1,0},{2,3},{3,2},{4,5},{5,4},{6,7},{7,6},{8,9},{9,8},{10,11... | collective-permute-start | bytes 393224 | tf_op jit(solution)/shard_map/ppermute | solution.py:30
  26.3 15.0 %collective-permute-start.3 = (f32[3,2,64,256]{3,2,1,0:T(8,128)S(1)}, f32[3,2,64,256]{3,2,1,0:T(8,128)S(1)}, u32[]{:S(2)}, u32[]{:S(2)}) collective-permute-start(f32[3,2,64,256]{3,2,1,0:T(8,128)S(1)} %collective-permute-done.2.rest_0_), channel_id=1, source_target_pairs={{0,1},{1,0},{2,3},{3,2},{4,5},{5,4},{6,7},{7,6},{8,9},{9,8},{10,11... | collective-permute-start | bytes 1179656 | tf_op jit(solution)/shard_map/ppermute | solution.py:30
  26.8 8.4 %collective-permute-start.6 = (f32[2,2,64,128]{3,2,1,0:T(8,128)S(1)}, f32[2,2,64,128]{3,2,1,0:T(8,128)S(1)}, u32[]{:S(2)}, u32[]{:S(2)}) collective-permute-start(f32[2,2,64,128]{3,2,1,0:T(8,128)S(1)} %collective-permute-done.4.rest_2_), channel_id=1, source_target_pairs={{0,2},{2,0},{1,3},{3,1},{4,6},{6,4},{5,7},{7,5},{8,10},{10,8},{9,1... | collective-permute-start | bytes 393224 | tf_op jit(solution)/shard_map/ppermute | solution.py:30
  32.5 5.5 %collective-permute-start.10 = (f32[2,2,64,128]{3,2,1,0:T(8,128)S(1)}, f32[2,2,64,128]{3,2,1,0:T(8,128)S(1)}, u32[]{:S(2)}, u32[]{:S(2)}) collective-permute-start(f32[2,2,64,128]{3,2,1,0:T(8,128)S(1)} %collective-permute-done.8.rest_6_), channel_id=1, source_target_pairs={{0,2},{2,0},{1,3},{3,1},{4,6},{6,4},{5,7},{7,5},{8,10},{10,8},{9,1... | collective-permute-start | bytes 393224 | tf_op jit(solution)/shard_map/ppermute | solution.py:30
  32.5 6.9 %collective-permute-start.17 = (f32[2,2,64,128]{3,2,1,0:T(8,128)S(1)}, f32[2,2,64,128]{3,2,1,0:T(8,128)S(1)}, u32[]{:S(2)}, u32[]{:S(2)}) collective-permute-start(f32[2,2,64,128]{3,2,1,0:T(8,128)S(1)} %collective-permute-done.15.rest_6_), channel_id=1, source_target_pairs={{0,2},{2,0},{1,3},{3,1},{4,6},{6,4},{5,7},{7,5},{8,10},{10,8},{9,1... | collective-permute-start | bytes 393224 | tf_op jit(solution)/shard_map/ppermute | solution.py:30
  35.3 4.1 %collective-permute-start.16 = (f32[2,2,64,128]{3,2,1,0:T(8,128)S(1)}, f32[2,2,64,128]{3,2,1,0:T(8,128)S(1)}, u32[]{:S(2)}, u32[]{:S(2)}) collective-permute-start(f32[2,2,64,128]{3,2,1,0:T(8,128)S(1)} %collective-permute-done.15.rest_6_), channel_id=1, source_target_pairs={{0,1},{1,0},{2,3},{3,2},{4,5},{5,4},{6,7},{7,6},{8,9},{9,8},{10,11... | collective-permute-start | bytes 393224 | tf_op jit(solution)/shard_map/ppermute | solution.py:30
  38.0 1.9 %collective-permute-start.14 = (f32[2,2,64,128]{3,2,1,0:T(8,128)S(1)}, f32[2,2,64,128]{3,2,1,0:T(8,128)S(1)}, u32[]{:S(2)}, u32[]{:S(2)}) collective-permute-start(f32[2,2,64,128]{3,2,1,0:T(8,128)S(1)} %collective-permute-done.13.rest_4_), channel_id=1, source_target_pairs={{0,1},{1,0},{2,3},{3,2},{4,5},{5,4},{6,7},{7,6},{8,9},{9,8},{10,11... | collective-permute-start | bytes 393224 | tf_op jit(solution)/shard_map/ppermute | solution.py:30
  39.4 1.3 %collective-permute-start.18 = (f32[2,2,64,128]{3,2,1,0:T(8,128)S(1)}, f32[2,2,64,128]{3,2,1,0:T(8,128)S(1)}, u32[]{:S(2)}, u32[]{:S(2)}) collective-permute-start(f32[2,2,64,128]{3,2,1,0:T(8,128)S(1)} %collective-permute-done.17.rest_8_), channel_id=1, source_target_pairs={{0,1},{1,0},{2,3},{3,2},{4,5},{5,4},{6,7},{7,6},{8,9},{9,8},{10,11... | collective-permute-start | bytes 393224 | tf_op jit(solution)/shard_map/ppermute | solution.py:30
  39.4 7.3 %collective-permute-start.5 = (f32[2,2,64,128]{3,2,1,0:T(8,128)S(1)}, f32[2,2,64,128]{3,2,1,0:T(8,128)S(1)}, u32[]{:S(2)}, u32[]{:S(2)}) collective-permute-start(f32[2,2,64,128]{3,2,1,0:T(8,128)S(1)} %collective-permute-done.4.rest_2_), channel_id=1, source_target_pairs={{0,1},{1,0},{2,3},{3,2},{4,5},{5,4},{6,7},{7,6},{8,9},{9,8},{10,11... | collective-permute-start | bytes 393224 | tf_op jit(solution)/shard_map/ppermute | solution.py:30
  39.9 6.7 %collective-permute-start.9 = (f32[2,2,64,128]{3,2,1,0:T(8,128)S(1)}, f32[2,2,64,128]{3,2,1,0:T(8,128)S(1)}, u32[]{:S(2)}, u32[]{:S(2)}) collective-permute-start(f32[2,2,64,128]{3,2,1,0:T(8,128)S(1)} %collective-permute-done.8.rest_6_), channel_id=1, source_target_pairs={{0,1},{1,0},{2,3},{3,2},{4,5},{5,4},{6,7},{7,6},{8,9},{9,8},{10,11... | collective-permute-start | bytes 393224 | tf_op jit(solution)/shard_map/ppermute | solution.py:30
  40.7 5.9 %collective-permute-start.7 = (f32[2,2,64,128]{3,2,1,0:T(8,128)S(1)}, f32[2,2,64,128]{3,2,1,0:T(8,128)S(1)}, u32[]{:S(2)}, u32[]{:S(2)}) collective-permute-start(f32[2,2,64,128]{3,2,1,0:T(8,128)S(1)} %collective-permute-done.6.rest_4_), channel_id=1, source_target_pairs={{0,1},{1,0},{2,3},{3,2},{4,5},{5,4},{6,7},{7,6},{8,9},{9,8},{10,11... | collective-permute-start | bytes 393224 | tf_op jit(solution)/shard_map/ppermute | solution.py:30
  40.9 5.8 %collective-permute-start.11 = (f32[2,2,64,128]{3,2,1,0:T(8,128)S(1)}, f32[2,2,64,128]{3,2,1,0:T(8,128)S(1)}, u32[]{:S(2)}, u32[]{:S(2)}) collective-permute-start(f32[2,2,64,128]{3,2,1,0:T(8,128)S(1)} %collective-permute-done.10.rest_8_), channel_id=1, source_target_pairs={{0,1},{1,0},{2,3},{3,2},{4,5},{5,4},{6,7},{7,6},{8,9},{9,8},{10,11... | collective-permute-start | bytes 393224 | tf_op jit(solution)/shard_map/ppermute | solution.py:30
  (2 other events, 2.8 us)

commit v2 on v0

v2 whole, which is shorter than its diff:
```python
import functools
import math

import numpy as np

import jax
import jax.numpy as jnp
from jax import lax
from jax.experimental import pallas as pl
from jax.experimental.pallas import tpu as pltpu
from jax.sharding import PartitionSpec as P


f32 = jnp.float32
bf16 = jnp.bfloat16
VMEM = pl.BlockSpec(memory_space=pltpu.VMEM)
SMEM = pl.BlockSpec(memory_space=pltpu.SMEM)
HBM = pl.BlockSpec(memory_space=pltpu.HBM)


def in_hbm(value):
    return pltpu.with_memory_space_constraint(value, pltpu.HBM)


def cut(value):
    high = value.astype(bf16)
    return high, (value - high.astype(f32)).astype(bf16)


def three_pass(left, right, dims):
    def dot(a, b):
        return lax.dot_general(a, b, (dims, ((), ())), preferred_element_type=f32)

    return dot(left[0], right[0]) + dot(left[0], right[1]) + dot(left[1], right[0])


def place(axes):
    return jnp.stack([lax.axis_index(axis) for axis in axes]).astype(jnp.int32)


def partner(value, axis, distance):
    size = lax.axis_size(axis)
    return lax.ppermute(value, axis, [(i, i ^ distance) for i in range(size)])


def pack_body(first, where, peram, together, *rest):
    outs, sems = rest[:-1], rest[-1]
    copies = []
    for distance, out in enumerate(outs):
        tslice = where[1] ^ distance
        targets = [out]
        if distance in first:
            targets.append(together.at[first.index(distance)])
        for target in targets:
            copies.append(pltpu.make_async_copy(peram.at[:, tslice], target, sems.at[len(copies)]))
            copies[-1].start()
    for copy in copies:
        copy.wait()


def pack(where, peram, first):
    parts, times = peram.shape[:2]
    one = (parts,) + peram.shape[2:]
    return pl.pallas_call(
        functools.partial(pack_body, first),
        out_shape=[jax.ShapeDtypeStruct(dims, f32) for dims in [(len(first),) + one] + [one] * times],
        in_specs=[SMEM, HBM],
        out_specs=[VMEM] * (times + 1),
        scratch_shapes=[pltpu.SemaphoreType.DMA((times + len(first),))],
        name="pack",
        cost_estimate=pl.CostEstimate(flops=0, bytes_accessed=peram.size * 12, transcendentals=0),
        compiler_params=pltpu.CompilerParams(vmem_limit_bytes=8 << 20),
    )(where, in_hbm(peram))


def sums_body(
    chips, cores, where, vectors, moved, v_other, d_other, own, other, v_buf, d_buf, left_high, left_low, v_sem, d_sem
):
    colours, sites, width = vectors.shape[2:]
    kinds = moved.shape[1]
    depth = colours * sites
    rows = width // (chips * cores)
    kind = pl.program_id(0)

    def v_copy(colour):
        return pltpu.make_async_copy(vectors.at[:, 0, colour], v_buf.at[colour], v_sem.at[colour])

    def d_copy(index):
        return pltpu.make_async_copy(moved.at[:, index, 0], d_buf.at[index], d_sem.at[index])

    @pl.when(kind == 0)
    def _():
        for colour in range(colours):
            v_copy(colour).start()
        for index in range(kinds):
            d_copy(index).start()
        spots = [(chip ^ where[2]) * rows for chip in range(chips)]
        for source in range(cores - 1, -1, -1):
            for colour in range(colours):
                if source == 0:
                    v_copy(colour).wait()
                    pair = v_buf[colour, 0].T, v_buf[colour, 1].T
                else:
                    pair = v_other[0, 0, colour].T, v_other[1, 0, colour].T
                at = source * 2 * depth + colour * sites
                for chip, spot in enumerate(spots):
                    base = chip * cores * rows
                    real, imag = [
                        jnp.where(where[3] == 0, value[base : base + rows], value[base + rows : base + 2 * rows])
                        for value in pair
                    ]
                    for scratch, re, im in zip((left_high, left_low), cut(real), cut(imag)):
                        for part, col, value in ((0, at, re), (0, depth + at, im), (1, at, -im), (1, depth + at, re)):
                            to = pl.multiple_of(part * chips * rows + spot, rows)
                            scratch[pl.ds(to, rows), col : col + sites] = value

    d_copy(kind).wait()
    result = None
    for source in range(cores):
        value = d_buf[kind] if source == 0 else d_other[:, kind, 0]
        at = slice(source * 2 * depth, (source + 1) * 2 * depth)
        term = three_pass((left_high[:, at], left_low[:, at]), cut(value.reshape(2 * depth, width)), ((1,), (0,)))
        result = term if result is None else result + term
    for part in range(2):
        at = part * chips * rows
        own[0, part] = result[at : at + rows]
        for away in range(chips - 1):
            at += rows
            other[0, away, part] = result[at : at + rows]


def sums(where, vectors, displaced, v_other, d_other, chips, cores):
    colours, sites, width = vectors.shape[2:]
    kinds = displaced.shape[1]
    rows = width // (chips * cores)
    depth = 2 * colours * sites
    own = jax.ShapeDtypeStruct((kinds, 2, rows, width), f32)
    other = jax.ShapeDtypeStruct((kinds, chips - 1, 2, rows, width), f32)
    return pl.pallas_call(
        functools.partial(sums_body, chips, cores),
        out_shape=[own, other],
        grid=(kinds,),
        in_specs=[SMEM, HBM, HBM, VMEM, VMEM],
        out_specs=[
            pl.BlockSpec((1,) + own.shape[1:], lambda i: (i, 0, 0, 0)),
            pl.BlockSpec((1,) + other.shape[1:], lambda i: (i, 0, 0, 0, 0)),
        ],
        scratch_shapes=[
            pltpu.VMEM((colours, 2, sites, width), f32),
            pltpu.VMEM((kinds, 2, colours, sites, width), f32),
            pltpu.VMEM((2 * chips * rows, cores * depth), bf16),
            pltpu.VMEM((2 * chips * rows, cores * depth), bf16),
            pltpu.SemaphoreType.DMA((colours,)),
            pltpu.SemaphoreType.DMA((kinds,)),
        ],
        name="sums",
        cost_estimate=pl.CostEstimate(
            flops=12 * width * depth * width * kinds,
            bytes_accessed=4 * (vectors.size + displaced.size) + 4 * kinds * 4 * width * width,
            transcendentals=0,
        ),
        compiler_params=pltpu.CompilerParams(vmem_limit_bytes=20 << 20, dimension_semantics=("arbitrary",)),
    )(where, in_hbm(vectors), in_hbm(displaced), v_other, d_other)


def mix_body(cores, where, gamma, pattern, mine, theirs, out_high, out_low, spread):
    operator = pl.program_id(0)
    times = mine.shape[0]
    per_core, cols, rows = mine.shape[2:]
    lanes = times * cols
    spins = cores * per_core
    sinks = spins // cores

    @pl.when(operator == 0)
    def _():
        for step in range(times):
            at = pl.multiple_of((where[1] ^ step) * cols, cols)
            for core, block in enumerate((mine, theirs)):
                for spin in range(per_core):
                    real = block[step, 0, spin]
                    imag = block[step, 1, spin]
                    for part, value in enumerate((real, imag, real + imag)):
                        spread[part, core * per_core + spin, pl.ds(at, cols), :] = value

    for sink in range(sinks):
        row = where[3] * sinks + sink
        totals = [None] * 3
        for core in range(cores):
            for spin in range(per_core):
                source = (where[3] ^ core) * per_core + spin
                on = pattern[operator, row, source].astype(f32)
                a = gamma[0, operator, row, source] * on
                b = gamma[1, operator, row, source] * on
                for index, (factor, part) in enumerate(((a, 2), (b - a, 0), (a + b, 1))):
                    term = factor * spread[part, core * per_core + spin]
                    totals[index] = term if totals[index] is None else totals[index] + term
        for part, value in enumerate((totals[0] - totals[2], totals[0] + totals[1])):
            high, low = cut(value)
            at = (slice(sink * lanes, (sink + 1) * lanes), slice(part * rows, (part + 1) * rows))
            out_high[(0,) + at] = high
            out_low[(0,) + at] = low


def mix(where, gamma, pattern, mine, theirs, cores):
    operators, spins = gamma.shape[1:3]
    cols, rows = mine.shape[-2:]
    lanes = mine.shape[0] * cols
    sinks = spins // cores
    out = jax.ShapeDtypeStruct((operators, sinks * lanes, 2 * rows), bf16)
    return pl.pallas_call(
        functools.partial(mix_body, cores),
        out_shape=[out, out],
        grid=(operators,),
        in_specs=[SMEM] * 3 + [VMEM] * 2,
        out_specs=[pl.BlockSpec((1,) + out.shape[1:], lambda o: (o, 0, 0))] * 2,
        scratch_shapes=[pltpu.VMEM((3, spins, lanes, rows), f32)],
        cost_estimate=pl.CostEstimate(
            flops=operators * sinks * spins * 8 * lanes * rows,
            bytes_accessed=4 * out.size + 8 * spins * lanes * rows,
            transcendentals=0,
        ),
        compiler_params=pltpu.CompilerParams(vmem_limit_bytes=12 << 20, dimension_semantics=("arbitrary",)),
    )(where, gamma, pattern, mine, theirs)


def phase(turns, chips, table):
    value = f32(table[0])
    for step in range(1, chips):
        value = jnp.where(turns == step, f32(table[step]), value)
    return value


def products_body(chips, cores, tables, where, directions, momenta, mine, theirs, *rest):
    far = rest[: chips - 1]
    far_other = rest[chips - 1 : 2 * (chips - 1)]
    mixed = rest[2 * (chips - 1) : -6]
    out, planes, e_high, e_low, staged, sems = rest[-6:]
    kinds, _, rows, width = mine.shape
    row_count = cores * rows
    operators = mixed[0].shape[0]
    sinks = out.shape[3]
    lanes = out.shape[5]
    depth_rows = width // chips

    for away in range(chips):
        plane = where[2] ^ away
        for kind in range(kinds):
            for part in range(2):
                for core in range(cores):
                    at = slice(core * rows, (core + 1) * rows)
                    if away == 0:
                        value = (mine, theirs)[core][kind, part]
                    else:
                        value = (far, far_other)[core][away - 1][kind, part]
                    planes[plane, kind, part, at] = value

    lane = lax.broadcasted_iota(jnp.int32, (row_count, width), 1)
    copies = []
    for operator in range(operators):
        kind = directions[operator]
        real = planes[0, kind, 0]
        imag = planes[0, kind, 1]
        for plane in range(1, chips):
            turns = lax.rem(momenta[operator] * plane, chips)
            cosine = phase(turns, chips, tables[0])
            sine = phase(turns, chips, tables[1])
            p_real = planes[plane, kind, 0]
            p_imag = planes[plane, kind, 1]
            real = real + (cosine * p_real + sine * p_imag)
            imag = imag + (cosine * p_imag - sine * p_real)
        bit = 1
        while bit < chips:
            reach = bit * depth_rows
            turned = []
            for value in (real, imag):
                up = pltpu.roll(value, width - reach, 1)
                down = up if 2 * reach == width else pltpu.roll(value, reach, 1)
                swapped = jnp.where((lane & reach) == 0, up, down)
                turned.append(jnp.where((where[2] & bit) != 0, swapped, value))
            real, imag = turned
            bit *= 2
        right_col = depth_rows
        for value, spots in ((real, ((0, 0, 1), (row_count, right_col, 1))), (imag, ((row_count, 0, 1), (0, right_col, -1)))):
            for scratch, piece in zip((e_high, e_low), cut(value)):
                for away in range(chips):
                    part = piece[:, away * depth_rows : (away + 1) * depth_rows]
                    for row, col, sign in spots:
                        scratch[operator, away, row : row + row_count, col : col + depth_rows] = part if sign > 0 else -part
        result = None
        for away in range(chips):
            left = (e_high[operator, away], e_low[operator, away])
            right = (mixed[2 * away][operator], mixed[2 * away + 1][operator])
            term = three_pass(left, right, ((1,), (1,)))
            result = term if result is None else result + term
        for part in range(2):
            for core in range(cores):
                row = pl.multiple_of((where[3] ^ core) * rows, rows)
                for sink in range(sinks):
                    staged[operator, part, sink, pl.ds(row, rows), :] = result[
                        part * row_count + core * rows : part * row_count + (core + 1) * rows,
                        sink * lanes : (sink + 1) * lanes,
                    ]
        copies.append(pltpu.make_async_copy(staged.at[operator], out.at[:, operator, 0], sems.at[operator]))
        copies[-1].start()
    for copy in copies:
        copy.wait()


def products(where, directions, momenta, mine, theirs, far, far_other, mixed, shape, chips, cores):
    kinds, width = mine.shape[0], mine.shape[3]
    rows = cores * mine.shape[2]
    tables = [
        [float(v) for v in fn(np.arange(chips, dtype=np.float32) * np.float32(2.0 * math.pi / chips))]
        for fn in (np.cos, np.sin)
    ]
    operands = [where, directions, momenta, mine, theirs, *far, *far_other, *mixed]
    return pl.pallas_call(
        functools.partial(products_body, chips, cores, tables),
        out_shape=jax.ShapeDtypeStruct(shape, f32),
        in_specs=[SMEM] * 3 + [VMEM] * (len(operands) - 3),
        out_specs=HBM,
        scratch_shapes=[
            pltpu.VMEM((chips, kinds, 2, rows, width), f32),
            pltpu.VMEM((shape[1], chips, 2 * rows, 2 * width // chips), bf16),
            pltpu.VMEM((shape[1], chips, 2 * rows, 2 * width // chips), bf16),
            pltpu.VMEM((shape[1], 2) + shape[3:], f32),
            pltpu.SemaphoreType.DMA((shape[1],)),
        ],
        name="products",
        cost_estimate=pl.CostEstimate(
            flops=3 * 2 * shape[1] * shape[3] * 2 * rows * 2 * width * shape[5],
            bytes_accessed=4 * math.prod(shape),
            transcendentals=0,
        ),
        compiler_params=pltpu.CompilerParams(vmem_limit_bytes=24 << 20),
    )(*operands)


def program(eigenvectors, displaced, perambulators, gamma_values, spin_pattern, directions, momenta):
    width = eigenvectors.shape[4]
    operators = gamma_values.shape[1]
    spins = gamma_values.shape[2]
    times = lax.axis_size("tm")
    chips = lax.axis_size("space")
    cores = lax.axis_size("spin")
    where = place(("parts", "tm", "space", "spin"))

    first = [d for d in range(times) if d == 0 or d % 2]
    later = [d for d in range(times) if d not in first]
    v_other = partner(eigenvectors, "spin", 1)
    d_other = partner(displaced, "spin", 1)
    together, *blocks = pack(where, jnp.swapaxes(perambulators, 3, 4), first)
    crossed = [partner(together, "space", away) for away in range(1, chips)]
    early = {}
    for d in range(1, times):
        early[d] = partner(blocks[d], "tm", d)
    own, other = sums(where, eigenvectors, displaced, v_other, d_other, chips, cores)
    far = [partner(other[:, away - 1], "space", away) for away in range(1, chips)]
    theirs = partner(own, "spin", 1)
    far_other = [partner(value, "spin", 1) for value in far]

    gathered = {}
    for d in first[1:]:
        gathered[d] = [partner(value[first.index(d)], "tm", d) for value in crossed]
    for d in later:
        gathered[d] = [partner(early[d], "space", away) for away in range(1, chips)]
    gathered[0] = [value[0] for value in crossed]
    mixed = []
    for away in range(chips):
        if away == 0:
            here = jnp.stack([blocks[0]] + [early[d] for d in range(1, times)])
        else:
            here = jnp.stack([gathered[d][away - 1] for d in range(times)])
        there = partner(here, "spin", 1)
        mixed += mix(where, gamma_values, spin_pattern, here, there, cores)
    shape = (2, operators, eigenvectors.shape[1], spins // cores, width // chips, perambulators.shape[4] * times)
    return products(where, directions, momenta, own, theirs, far, far_other, mixed, shape, chips, cores)


def solution(mesh):
    in_specs = (
        P(None, ("parts", "tm"), None, ("space", "spin"), None),
        P(None, None, ("parts", "tm"), None, ("space", "spin"), None),
        P(None, "parts", "spin", "space", "tm"),
        P(),
        P(),
        P(),
        P(),
    )
    out_specs = P(None, None, ("parts", "tm"), "spin", "space", None)
    return jax.shard_map(program, mesh=mesh, in_specs=in_specs, out_specs=out_specs, check_vma=False)
```

time: 137 us -> 43.1 us (0.31)
  matrix products: 36.8 us -> 0 us
  waiting for transfers between devices: 46.6 us -> 14 us
  between operations: 22.4 us -> 0.15 us
  local copies, waits for them, and re-layouts: 17.6 us -> 0.05 us
  Pallas kernels: 0 us -> 14.7 us
  starting transfers between devices: 6.66 us -> 14 us
  other arithmetic: 6.41 us -> 0.16 us
    reduce_scatter x1 -> x0, waiting for transfers between devices: 44.4 us -> none  [local(): lax.psum_scatter(pieces, ('space', 'spin'), scatter_dimension=0, tiled=True)]
    dot_general x9 -> x0, matrix products: 36.8 us -> none  [the longest x1 10.6 us: local(): lax.dot_general(left_rows, rights[tslice], (((0,), (0,)), ((), ())), prec...]
    pallas_call x0 -> x5, Pallas kernels: none -> 14.7 us  [the longest x1 4.85 us: sums(): pl.pallas_call(functools.partial(sums_body, chips, cores), out_shape=[own...]
    ppermute x0 -> x14, starting transfers between devices: none -> 14 us  [partner(): return lax.ppermute(value, axis, [(i, i ^ distance) for i in range(size)])]
    ppermute x0 -> x14, waiting for transfers between devices: none -> 14 us  [partner(): return lax.ppermute(value, axis, [(i, i ^ distance) for i in range(size)])]
    all_to_all x1 -> x0, starting transfers between devices: 6.35 us -> none  [local(): lax.all_to_all(perambulators, 'tm', split_axis=1, concat_axis=4, tiled=True)]
    all_gather x2 -> x0, local copies, waits for them, and re-layouts: 5.4 us -> none  [the longest x1 2.87 us: local(): arrived = lax.all_gather(arrived, 'spin', axis=2, tiled=True)]
    neg x1 -> x0, other arithmetic: 3.97 us -> none  [local(): -real_w]
  transfers between devices with their start and end apart: 5 -> 14, of which waited for: 2 -> 3; matrix products, arithmetic and copies ran while one was open for 32% -> 0% of each run, Pallas kernels for 0% -> 26%
where the time goes in v2:
time: 43.1 us; the launch traced here: 43 us
  Pallas kernels  14.7 us (34%)
  starting transfers between devices  14 us (32%)
  waiting for transfers between devices  14 us (32%)
    ppermute x14, starting transfers between devices, partner(): return lax.ppermute(value, axis, [(i, i ^ distance) for i in range(size)])  14 us
    ppermute x14, waiting for transfers between devices, partner(): return lax.ppermute(value, axis, [(i, i ^ distance) for i in range(size)])  14 us
    pallas_call x1, Pallas kernels, sums(): pl.pallas_call(functools.partial(sums_body, chips, cores), out_shape=[own...  4.85 us
    pallas_call x2, Pallas kernels, mix(): pl.pallas_call(functools.partial(mix_body, cores), out_shape=[out, out],...  4.65 us
    pallas_call x1, Pallas kernels, products(): pl.pallas_call(functools.partial(products_body, chips, cores, tables), ou...  3.37 us
    pallas_call x1, Pallas kernels, pack(): pl.pallas_call(functools.partial(pack_body, first), out_shape=[jax.ShapeD...  1.85 us
  transfers between devices with their start and end apart: 14, of which 3 were waited for; matrix products, arithmetic and copies ran while one was open for 0% of the time, Pallas kernels for 26%

profile of v2, /device:TPU:0, one launch (start us, length us, event | category | flops | bytes accessed | tf_op | source)
XLA Modules:
  0.0 43.0 jit_solution(5387630643580352854)
XLA Ops:
  0.0 0.5 %collective-permute-start.1 = (f32[2,3,1,3,128,256]{5,4,3,2,1,0:T(8,128)}, f32[2,3,1,3,128,256]{5,4,3,2,1,0:T(8,128)S(1)}, u32[]{:S(2)}, u32[]{:S(2)}) collective-permute-start(f32[2,3,1,3,128,256]{5,4,3,2,1,0:T(8,128)} %moved.1), channel_id=1, source_target_pairs={{0,1},{1,0},{2,3},{3,2},{4,5},{5,4},{6,7},{7,6},{8,9},{9,8},{10,11... | collective-permute-start | bytes 7077896 | tf_op jit(solution)/shard_map/ppermute | solution.py:43
  0.5 0.0 collective-permute-start
  0.5 0.1 pad_add_fusion.where
  0.6 1.8 %pack.1 = (f32[3,2,2,64,128]{4,3,2,1,0:T(8,128)S(1)}, f32[2,2,64,128]{3,2,1,0:T(8,128)S(1)}, f32[2,2,64,128]{3,2,1,0:T(8,128)S(1)}, f32[2,2,64,128]{3,2,1,0:T(8,128)S(1)}, f32[2,2,64,128]{3,2,1,0:T(8,128)S(1)}) custom-call(s32[4]{0:T(128)S(1)} %pad_add_fusion.where, f32[2,4,2,64,128]{4,3,2,1,0:T(8,128)} %bitcast.19), custom_call_target="tpu_custom_call" | custom-call | bytes 1572864 | tf_op jit(solution)/shard_map/pack/pallas_call | solution.py:64
  2.4 3.0 %collective-permute-start.9 = (f32[3,2,2,64,128]{4,3,2,1,0:T(8,128)S(1)}, f32[3,2,2,64,128]{4,3,2,1,0:T(8,128)S(1)}, u32[]{:S(2)}, u32[]{:S(2)}) collective-permute-start(f32[3,2,2,64,128]{4,3,2,1,0:T(8,128)S(1)} %get-tuple-element.24), channel_id=1, source_target_pairs={{0,2},{2,0},{1,3},{3,1},{4,6},{6,4},{5,7},{7,5},{8,10},{10,8},{9,1... | collective-permute-start | bytes 1179656 | tf_op jit(solution)/shard_map/ppermute | solution.py:43
  5.5 2.6 %collective-permute-start.6 = (f32[2,2,64,128]{3,2,1,0:T(8,128)S(1)}, f32[2,2,64,128]{3,2,1,0:T(8,128)S(1)}, u32[]{:S(2)}, u32[]{:S(2)}) collective-permute-start(f32[2,2,64,128]{3,2,1,0:T(8,128)S(1)} %get-tuple-element.20), channel_id=1, source_target_pairs={{0,8},{4,12},{8,0},{12,4},{1,9},{5,13},{9,1},{13,5},{2,10},{6,14},... | collective-permute-start | bytes 393224 | tf_op jit(solution)/shard_map/ppermute | solution.py:43
  8.1 1.3 %collective-permute-start.7 = (f32[2,2,64,128]{3,2,1,0:T(8,128)S(1)}, f32[2,2,64,128]{3,2,1,0:T(8,128)S(1)}, u32[]{:S(2)}, u32[]{:S(2)}) collective-permute-start(f32[2,2,64,128]{3,2,1,0:T(8,128)S(1)} %get-tuple-element.21), channel_id=1, source_target_pairs={{0,12},{4,8},{8,4},{12,0},{1,13},{5,9},{9,5},{13,1},{2,14},{6,10},... | collective-permute-start | bytes 393224 | tf_op jit(solution)/shard_map/ppermute | solution.py:43
  9.4 8.8 %collective-permute-done.6 = f32[2,2,64,128]{3,2,1,0:T(8,128)S(1)} collective-permute-done((f32[2,2,64,128]{3,2,1,0:T(8,128)S(1)}, f32[2,2,64,128]{3,2,1,0:T(8,128)S(1)}, u32[]{:S(2)}, u32[]{:S(2)}) %collective-permute-start.6) | collective-permute-done | bytes 131104 | tf_op jit(solution)/shard_map/ppermute | solution.py:43
  18.2 0.3 collective-permute-start.11
  18.6 4.9 %sums.1 = (f32[3,2,64,256]{3,2,1,0:T(8,128)S(1)}, f32[3,1,2,64,256]{4,3,2,1,0:T(8,128)S(1)}) custom-call(s32[4]{0:T(128)S(1)} %pad_add_fusion.where, f32[2,1,3,128,256]{4,3,2,1,0:T(8,128)} %vectors.1, f32[2,3,1,3,128,256]{5,4,3,2,1,0:T(8,128)} %moved.1, f32[2,1,3,128,256]{4,3,2,1,0:T(8,128)S(1)} %collective-permute-done.v_other, ...), custom_call_target="tpu_custom_call" | custom-call | flops 1811939328 | bytes 6291456 | tf_op jit(solution)/shard_map/sums/pallas_call | solution.py:139
  23.4 0.0 copy-start
  23.5 0.0 copy-start.3
  23.5 1.8 %collective-permute-start.3 = (f32[3,2,64,256]{3,2,1,0:T(8,128)S(1)}, f32[3,2,64,256]{3,2,1,0:T(8,128)S(1)}, u32[]{:S(2)}, u32[]{:S(2)}) collective-permute-start(f32[3,2,64,256]{3,2,1,0:T(8,128)S(1)} %bitcast.18), channel_id=1, source_target_pairs={{0,2},{2,0},{1,3},{3,1},{4,6},{6,4},{5,7},{7,5},{8,10},{10,8},{9,1... | collective-permute-start | bytes 1179656 | tf_op jit(solution)/shard_map/ppermute | solution.py:43
  25.3 2.5 %collective-permute-start.12 = (f32[2,2,64,128]{3,2,1,0:T(8,128)S(1)}, f32[2,2,64,128]{3,2,1,0:T(8,128)S(1)}, u32[]{:S(2)}, u32[]{:S(2)}) collective-permute-start(f32[2,2,64,128]{3,2,1,0:T(8,128)S(1)} %get-tuple-element.28), channel_id=1, source_target_pairs={{0,12},{4,8},{8,4},{12,0},{1,13},{5,9},{9,5},{13,1},{2,14},{6,10},... | collective-permute-start | bytes 393224 | tf_op jit(solution)/shard_map/ppermute | solution.py:43
  27.8 1.1 %collective-permute-start.10 = (f32[2,2,64,128]{3,2,1,0:T(8,128)S(1)}, f32[2,2,64,128]{3,2,1,0:T(8,128)S(1)}, u32[]{:S(2)}, u32[]{:S(2)}) collective-permute-start(f32[2,2,64,128]{3,2,1,0:T(8,128)S(1)} %get-tuple-element.29), channel_id=1, source_target_pairs={{0,4},{4,0},{8,12},{12,8},{1,5},{5,1},{9,13},{13,9},{2,6},{6,2},{1... | collective-permute-start | bytes 393224 | tf_op jit(solution)/shard_map/ppermute | solution.py:43
  29.0 0.1 collective-permute-start.8
  29.1 3.8 %collective-permute-done.12 = f32[2,2,64,128]{3,2,1,0:T(8,128)S(1)} collective-permute-done((f32[2,2,64,128]{3,2,1,0:T(8,128)S(1)}, f32[2,2,64,128]{3,2,1,0:T(8,128)S(1)}, u32[]{:S(2)}, u32[]{:S(2)}) %collective-permute-start.12) | collective-permute-done | bytes 131104 | tf_op jit(solution)/shard_map/ppermute | solution.py:43
  32.8 1.4 %collective-permute-done.10 = f32[2,2,64,128]{3,2,1,0:T(8,128)S(1)} collective-permute-done((f32[2,2,64,128]{3,2,1,0:T(8,128)S(1)}, f32[2,2,64,128]{3,2,1,0:T(8,128)S(1)}, u32[]{:S(2)}, u32[]{:S(2)}) %collective-permute-start.10) | collective-permute-done | bytes 131104 | tf_op jit(solution)/shard_map/ppermute | solution.py:43
  34.2 0.1 collective-permute-start.13
  34.3 0.5 %collective-permute-start.2 = (f32[3,2,64,256]{3,2,1,0:T(8,128)S(1)}, f32[3,2,64,256]{3,2,1,0:T(8,128)S(1)}, u32[]{:S(2)}, u32[]{:S(2)}) collective-permute-start(f32[3,2,64,256]{3,2,1,0:T(8,128)S(1)} %get-tuple-element.16.mine), channel_id=1, source_target_pairs={{0,1},{1,0},{2,3},{3,2},{4,5},{5,4},{6,7},{7,6},{8,9},{9,8},{10,11... | collective-permute-start | bytes 1179656 | tf_op jit(solution)/shard_map/ppermute | solution.py:43
  34.8 0.1 collective-permute-start.4
  34.9 2.3 %shard_map.73 = (bf16[4,512,256]{2,1,0:T(8,128)(2,1)S(1)}, bf16[4,512,256]{2,1,0:T(8,128)(2,1)S(1)}) custom-call(s32[4]{0:T(128)S(1)} %pad_add_fusion.where, f32[2,4,4,4]{3,2,1,0:T(4,128)S(1)} %copy-done, s32[4,4,4]{2,1,0:T(4,128)S(1)} %copy-done.1, f32[4,2,2,64,128]{4,3,2,1,0:T(8,128)S(1)} %pad_maximum_fusion.mine, ...), custom_call_target="tpu_custom_call" | custom-call | flops 8388608 | bytes 3145728 | tf_op jit(solution)/shard_map/pallas_call | solution.py:210
  37.2 2.3 %shard_map.74 = (bf16[4,512,256]{2,1,0:T(8,128)(2,1)S(1)}, bf16[4,512,256]{2,1,0:T(8,128)(2,1)S(1)}) custom-call(s32[4]{0:T(128)S(1)} %pad_add_fusion.where, f32[2,4,4,4]{3,2,1,0:T(4,128)S(1)} %copy-done, s32[4,4,4]{2,1,0:T(4,128)S(1)} %copy-done.1, f32[4,2,2,64,128]{4,3,2,1,0:T(8,128)S(1)} %pad_maximum_fusion.1.mine, ...), custom_call_target="tpu_custom_call" | custom-call | flops 8388608 | bytes 3145728 | tf_op jit(solution)/shard_map/pallas_call | solution.py:210
  39.6 3.4 %products.1 = f32[2,4,1,2,128,256]{5,4,3,2,1,0:T(8,128)} custom-call(s32[4]{0:T(128)S(1)} %pad_add_fusion.where, s32[4]{0:T(128)S(1)} %copy-done.2, s32[4]{0:T(128)S(1)} %copy-done.3, f32[3,2,64,256]{3,2,1,0:T(8,128)S(1)} %get-tuple-element.16.mine, f32[3,2,64,256]{3,2,1,0:T(8,128)S(1)} %collective-permute-done.2.theirs, ...), custom_call_target="tpu_custom_call" | custom-call | flops 1610612736 | bytes 2097152 | tf_op jit(solution)/shard_map/products/pallas_call | solution.py:317
  (21 shorter events, 0.2 us)
Async XLA Ops:
  0.0 18.6 %collective-permute-start.1 = (f32[2,3,1,3,128,256]{5,4,3,2,1,0:T(8,128)}, f32[2,3,1,3,128,256]{5,4,3,2,1,0:T(8,128)S(1)}, u32[]{:S(2)}, u32[]{:S(2)}) collective-permute-start(f32[2,3,1,3,128,256]{5,4,3,2,1,0:T(8,128)} %moved.1), channel_id=1, source_target_pairs={{0,1},{1,0},{2,3},{3,2},{4,5},{5,4},{6,7},{7,6},{8,9},{9,8},{10,11... | collective-permute-start | bytes 7077896 | tf_op jit(solution)/shard_map/ppermute | solution.py:43
  0.5 17.7 %collective-permute-start = (f32[2,1,3,128,256]{4,3,2,1,0:T(8,128)}, f32[2,1,3,128,256]{4,3,2,1,0:T(8,128)S(1)}, u32[]{:S(2)}, u32[]{:S(2)}) collective-permute-start(f32[2,1,3,128,256]{4,3,2,1,0:T(8,128)} %vectors.1), channel_id=1, source_target_pairs={{0,1},{1,0},{2,3},{3,2},{4,5},{5,4},{6,7},{7,6},{8,9},{9,8},{10,11... | collective-permute-start | bytes 2359304 | tf_op jit(solution)/shard_map/ppermute | solution.py:43
  2.4 22.8 %collective-permute-start.9 = (f32[3,2,2,64,128]{4,3,2,1,0:T(8,128)S(1)}, f32[3,2,2,64,128]{4,3,2,1,0:T(8,128)S(1)}, u32[]{:S(2)}, u32[]{:S(2)}) collective-permute-start(f32[3,2,2,64,128]{4,3,2,1,0:T(8,128)S(1)} %get-tuple-element.24), channel_id=1, source_target_pairs={{0,2},{2,0},{1,3},{3,1},{4,6},{6,4},{5,7},{7,5},{8,10},{10,8},{9,1... | collective-permute-start | bytes 1179656 | tf_op jit(solution)/shard_map/ppermute | solution.py:43
  5.5 12.8 %collective-permute-start.6 = (f32[2,2,64,128]{3,2,1,0:T(8,128)S(1)}, f32[2,2,64,128]{3,2,1,0:T(8,128)S(1)}, u32[]{:S(2)}, u32[]{:S(2)}) collective-permute-start(f32[2,2,64,128]{3,2,1,0:T(8,128)S(1)} %get-tuple-element.20), channel_id=1, source_target_pairs={{0,8},{4,12},{8,0},{12,4},{1,9},{5,13},{9,1},{13,5},{2,10},{6,14},... | collective-permute-start | bytes 393224 | tf_op jit(solution)/shard_map/ppermute | solution.py:43
  8.1 19.8 %collective-permute-start.7 = (f32[2,2,64,128]{3,2,1,0:T(8,128)S(1)}, f32[2,2,64,128]{3,2,1,0:T(8,128)S(1)}, u32[]{:S(2)}, u32[]{:S(2)}) collective-permute-start(f32[2,2,64,128]{3,2,1,0:T(8,128)S(1)} %get-tuple-element.21), channel_id=1, source_target_pairs={{0,12},{4,8},{8,4},{12,0},{1,13},{5,9},{9,5},{13,1},{2,14},{6,10},... | collective-permute-start | bytes 393224 | tf_op jit(solution)/shard_map/ppermute | solution.py:43
  18.2 10.7 %collective-permute-start.5 = (f32[2,2,64,128]{3,2,1,0:T(8,128)S(1)}, f32[2,2,64,128]{3,2,1,0:T(8,128)S(1)}, u32[]{:S(2)}, u32[]{:S(2)}) collective-permute-start(f32[2,2,64,128]{3,2,1,0:T(8,128)S(1)} %get-tuple-element.19), channel_id=1, source_target_pairs={{0,4},{4,0},{8,12},{12,8},{1,5},{5,1},{9,13},{13,9},{2,6},{6,2},{1... | collective-permute-start | bytes 393224 | tf_op jit(solution)/shard_map/ppermute | solution.py:43
  18.2 10.8 %collective-permute-start.11 = (f32[2,2,64,128]{3,2,1,0:T(8,128)S(1)}, f32[2,2,64,128]{3,2,1,0:T(8,128)S(1)}, u32[]{:S(2)}, u32[]{:S(2)}) collective-permute-start(f32[2,2,64,128]{3,2,1,0:T(8,128)S(1)} %collective-permute-done.6), channel_id=1, source_target_pairs={{0,2},{2,0},{1,3},{3,1},{4,6},{6,4},{5,7},{7,5},{8,10},{10,8},{9,1... | collective-permute-start | bytes 393224 | tf_op jit(solution)/shard_map/ppermute | solution.py:43
  23.4 11.5 %copy-start = (f32[2,4,4,4]{3,2,1,0:T(4,128)S(1)}, f32[2,4,4,4]{3,2,1,0:T(4,128)}, u32[]{:S(2)}) copy-start(f32[2,4,4,4]{3,2,1,0:T(4,128)} %gamma.3) | copy-start | bytes 1540
  23.4 11.5 %copy-start.1 = (s32[4,4,4]{2,1,0:T(4,128)S(1)}, s32[4,4,4]{2,1,0:T(4,128)}, u32[]{:S(2)}) copy-start(s32[4,4,4]{2,1,0:T(4,128)} %pattern.3) | copy-start | bytes 772
  23.5 16.1 %copy-start.2 = (s32[4]{0:T(128)S(1)}, s32[4]{0:T(128)}, u32[]{:S(2)}) copy-start(s32[4]{0:T(128)} %directions.1) | copy-start | bytes 52
  23.5 16.1 %copy-start.3 = (s32[4]{0:T(128)S(1)}, s32[4]{0:T(128)}, u32[]{:S(2)}) copy-start(s32[4]{0:T(128)} %momenta.1) | copy-start | bytes 52
  23.5 11.3 %collective-permute-start.3 = (f32[3,2,64,256]{3,2,1,0:T(8,128)S(1)}, f32[3,2,64,256]{3,2,1,0:T(8,128)S(1)}, u32[]{:S(2)}, u32[]{:S(2)}) collective-permute-start(f32[3,2,64,256]{3,2,1,0:T(8,128)S(1)} %bitcast.18), channel_id=1, source_target_pairs={{0,2},{2,0},{1,3},{3,1},{4,6},{6,4},{5,7},{7,5},{8,10},{10,8},{9,1... | collective-permute-start | bytes 1179656 | tf_op jit(solution)/shard_map/ppermute | solution.py:43
  25.3 7.6 %collective-permute-start.12 = (f32[2,2,64,128]{3,2,1,0:T(8,128)S(1)}, f32[2,2,64,128]{3,2,1,0:T(8,128)S(1)}, u32[]{:S(2)}, u32[]{:S(2)}) collective-permute-start(f32[2,2,64,128]{3,2,1,0:T(8,128)S(1)} %get-tuple-element.28), channel_id=1, source_target_pairs={{0,12},{4,8},{8,4},{12,0},{1,13},{5,9},{9,5},{13,1},{2,14},{6,10},... | collective-permute-start | bytes 393224 | tf_op jit(solution)/shard_map/ppermute | solution.py:43
  27.8 6.4 %collective-permute-start.10 = (f32[2,2,64,128]{3,2,1,0:T(8,128)S(1)}, f32[2,2,64,128]{3,2,1,0:T(8,128)S(1)}, u32[]{:S(2)}, u32[]{:S(2)}) collective-permute-start(f32[2,2,64,128]{3,2,1,0:T(8,128)S(1)} %get-tuple-element.29), channel_id=1, source_target_pairs={{0,4},{4,0},{8,12},{12,8},{1,5},{5,1},{9,13},{13,9},{2,6},{6,2},{1... | collective-permute-start | bytes 393224 | tf_op jit(solution)/shard_map/ppermute | solution.py:43
  29.0 5.9 %collective-permute-start.8 = (f32[4,2,2,64,128]{4,3,2,1,0:T(8,128)S(1)}, f32[4,2,2,64,128]{4,3,2,1,0:T(8,128)S(1)}, u32[]{:S(2)}, u32[]{:S(2)}) collective-permute-start(f32[4,2,2,64,128]{4,3,2,1,0:T(8,128)S(1)} %pad_maximum_fusion.mine), channel_id=1, source_target_pairs={{0,1},{1,0},{2,3},{3,2},{4,5},{5,4},{6,7},{7,6},{8,9},{9,8},{10,11... | collective-permute-start | bytes 1572872 | tf_op jit(solution)/shard_map/ppermute | solution.py:43
  34.2 3.0 %collective-permute-start.13 = (f32[4,2,2,64,128]{4,3,2,1,0:T(8,128)S(1)}, f32[4,2,2,64,128]{4,3,2,1,0:T(8,128)S(1)}, u32[]{:S(2)}, u32[]{:S(2)}) collective-permute-start(f32[4,2,2,64,128]{4,3,2,1,0:T(8,128)S(1)} %pad_maximum_fusion.1.mine), channel_id=1, source_target_pairs={{0,1},{1,0},{2,3},{3,2},{4,5},{5,4},{6,7},{7,6},{8,9},{9,8},{10,11... | collective-permute-start | bytes 1572872 | tf_op jit(solution)/shard_map/ppermute | solution.py:43
  34.3 5.3 %collective-permute-start.2 = (f32[3,2,64,256]{3,2,1,0:T(8,128)S(1)}, f32[3,2,64,256]{3,2,1,0:T(8,128)S(1)}, u32[]{:S(2)}, u32[]{:S(2)}) collective-permute-start(f32[3,2,64,256]{3,2,1,0:T(8,128)S(1)} %get-tuple-element.16.mine), channel_id=1, source_target_pairs={{0,1},{1,0},{2,3},{3,2},{4,5},{5,4},{6,7},{7,6},{8,9},{9,8},{10,11... | collective-permute-start | bytes 1179656 | tf_op jit(solution)/shard_map/ppermute | solution.py:43
  34.8 4.8 %collective-permute-start.4 = (f32[3,2,64,256]{3,2,1,0:T(8,128)S(1)}, f32[3,2,64,256]{3,2,1,0:T(8,128)S(1)}, u32[]{:S(2)}, u32[]{:S(2)}) collective-permute-start(f32[3,2,64,256]{3,2,1,0:T(8,128)S(1)} %collective-permute-done.3.rest_0_), channel_id=1, source_target_pairs={{0,1},{1,0},{2,3},{3,2},{4,5},{5,4},{6,7},{7,6},{8,9},{9,8},{10,11... | collective-permute-start | bytes 1179656 | tf_op jit(solution)/shard_map/ppermute | solution.py:43

commit v3 on v2

--- a/solution.py
+++ b/solution.py
@@ -44,18 +44,16 @@
 
 
 def pack_body(first, where, peram, together, *rest):
-    outs, sems = rest[:-1], rest[-1]
-    copies = []
+    outs, buffer, sem = rest[:-2], rest[-2], rest[-1]
+    copy = pltpu.make_async_copy(peram, buffer, sem)
+    copy.start()
+    copy.wait()
     for distance, out in enumerate(outs):
-        tslice = where[1] ^ distance
-        targets = [out]
-        if distance in first:
-            targets.append(together.at[first.index(distance)])
-        for target in targets:
-            copies.append(pltpu.make_async_copy(peram.at[:, tslice], target, sems.at[len(copies)]))
-            copies[-1].start()
-    for copy in copies:
-        copy.wait()
+        for part in range(buffer.shape[0]):
+            block = buffer[part, where[1] ^ distance]
+            out[part] = block
+            if distance in first:
+                together[first.index(distance), part] = block
 
 
 def pack(where, peram, first):
@@ -66,7 +64,7 @@
         out_shape=[jax.ShapeDtypeStruct(dims, f32) for dims in [(len(first),) + one] + [one] * times],
         in_specs=[SMEM, HBM],
         out_specs=[VMEM] * (times + 1),
-        scratch_shapes=[pltpu.SemaphoreType.DMA((times + len(first),))],
+        scratch_shapes=[pltpu.VMEM(peram.shape, f32), pltpu.SemaphoreType.DMA],
         name="pack",
         cost_estimate=pl.CostEstimate(flops=0, bytes_accessed=peram.size * 12, transcendentals=0),
         compiler_params=pltpu.CompilerParams(vmem_limit_bytes=8 << 20),
@@ -163,64 +161,74 @@
     )(where, in_hbm(vectors), in_hbm(displaced), v_other, d_other)
 
 
-def mix_body(cores, where, gamma, pattern, mine, theirs, out_high, out_low, spread):
-    operator = pl.program_id(0)
-    times = mine.shape[0]
-    per_core, cols, rows = mine.shape[2:]
-    lanes = times * cols
-    spins = cores * per_core
+def spread_out(blocks, spread):
+    per_core = blocks[0].shape[2]
+    for step in range(blocks[0].shape[0]):
+        for core, block in enumerate(blocks):
+            for spin in range(per_core):
+                real = block[step, 0, spin]
+                imag = block[step, 1, spin]
+                for part, value in enumerate((real, imag, real + imag)):
+                    spread[step, part, core * per_core + spin] = value
+
+
+def mix_one(steps, where, gamma, pattern, operator, spread, out_high, out_low):
+    spins, cols, rows = spread.shape[2:]
+    sinks = out_high.shape[1]
+    cores = spins // sinks
+    for index, step in enumerate(steps):
+        place = pl.ds(pl.multiple_of((where[1] ^ step) * cols, cols), cols)
+        for sink in range(sinks):
+            row = where[3] * sinks + sink
+            totals = [None] * 3
+            for core in range(cores):
+                for spin in range(sinks):
+                    source = (where[3] ^ core) * sinks + spin
+                    on = pattern[operator, row, source].astype(f32)
+                    a = gamma[0, operator, row, source] * on
+                    b = gamma[1, operator, row, source] * on
+                    for total, (factor, part) in enumerate(((a, 2), (b - a, 0), (a + b, 1))):
+                        term = factor * spread[index, part, core * sinks + spin]
+                        totals[total] = term if totals[total] is None else totals[total] + term
+            for part, value in enumerate((totals[0] - totals[2], totals[0] + totals[1])):
+                high, low = cut(value)
+                out_high[operator, sink, place, part * rows : (part + 1) * rows] = high
+                out_low[operator, sink, place, part * rows : (part + 1) * rows] = low
+
+
+def mix_body(steps, where, gamma, pattern, mine, theirs, out_high, out_low, spread):
+    spread_out((mine, theirs), spread)
+
+    def one(operator, carry):
+        mix_one(steps, where, gamma, pattern, operator, spread, out_high, out_low)
+        return carry
+
+    lax.fori_loop(0, gamma.shape[1], one, 0)
+
+
+def mix(where, gamma, pattern, mine, theirs, steps, times, cores):
+    operators, spins = gamma.shape[1:3]
+    count, _, _, cols, rows = mine.shape
     sinks = spins // cores
-
-    @pl.when(operator == 0)
-    def _():
-        for step in range(times):
-            at = pl.multiple_of((where[1] ^ step) * cols, cols)
-            for core, block in enumerate((mine, theirs)):
-                for spin in range(per_core):
-                    real = block[step, 0, spin]
-                    imag = block[step, 1, spin]
-                    for part, value in enumerate((real, imag, real + imag)):
-                        spread[part, core * per_core + spin, pl.ds(at, cols), :] = value
-
-    for sink in range(sinks):
-        row = where[3] * sinks + sink
-        totals = [None] * 3
-        for core in range(cores):
-            for spin in range(per_core):
-                source = (where[3] ^ core) * per_core + spin
-                on = pattern[operator, row, source].astype(f32)
-                a = gamma[0, operator, row, source] * on
-                b = gamma[1, operator, row, source] * on
-                for index, (factor, part) in enumerate(((a, 2), (b - a, 0), (a + b, 1))):
-                    term = factor * spread[part, core * per_core + spin]
-                    totals[index] = term if totals[index] is None else totals[index] + term
-        for part, value in enumerate((totals[0] - totals[2], totals[0] + totals[1])):
-            high, low = cut(value)
-            at = (slice(sink * lanes, (sink + 1) * lanes), slice(part * rows, (part + 1) * rows))
-            out_high[(0,) + at] = high
-            out_low[(0,) + at] = low
-
-
-def mix(where, gamma, pattern, mine, theirs, cores):
-    operators, spins = gamma.shape[1:3]
-    cols, rows = mine.shape[-2:]
-    lanes = mine.shape[0] * cols
-    sinks = spins // cores
-    out = jax.ShapeDtypeStruct((operators, sinks * lanes, 2 * rows), bf16)
+    out = jax.ShapeDtypeStruct((operators, sinks, times * cols, 2 * rows), bf16)
     return pl.pallas_call(
-        functools.partial(mix_body, cores),
+        functools.partial(mix_body, steps),
         out_shape=[out, out],
-        grid=(operators,),
         in_specs=[SMEM] * 3 + [VMEM] * 2,
-        out_specs=[pl.BlockSpec((1,) + out.shape[1:], lambda o: (o, 0, 0))] * 2,
-        scratch_shapes=[pltpu.VMEM((3, spins, lanes, rows), f32)],
+        out_specs=[VMEM] * 2,
+        scratch_shapes=[pltpu.VMEM((count, 3, spins, cols, rows), f32)],
+        name="mix",
         cost_estimate=pl.CostEstimate(
-            flops=operators * sinks * spins * 8 * lanes * rows,
-            bytes_accessed=4 * out.size + 8 * spins * lanes * rows,
+            flops=operators * sinks * spins * 8 * count * cols * rows,
+            bytes_accessed=4 * out.size,
             transcendentals=0,
         ),
-        compiler_params=pltpu.CompilerParams(vmem_limit_bytes=12 << 20, dimension_semantics=("arbitrary",)),
+        compiler_params=pltpu.CompilerParams(vmem_limit_bytes=8 << 20),
     )(where, gamma, pattern, mine, theirs)
+
+
+def flat(value):
+    return value.reshape((-1,) + value.shape[2:])
 
 
 def phase(turns, chips, table):
@@ -230,18 +238,29 @@
     return value
 
 
-def products_body(chips, cores, tables, where, directions, momenta, mine, theirs, *rest):
-    far = rest[: chips - 1]
-    far_other = rest[chips - 1 : 2 * (chips - 1)]
-    mixed = rest[2 * (chips - 1) : -6]
-    out, planes, e_high, e_low, staged, sems = rest[-6:]
+def products_body(
+    chips, cores, steps, tables, where, gamma, pattern, directions, momenta, mine, theirs, near_high, near_low, *rest
+):
+    away_count = chips - 1
+    far, far_other, late, late_other = [rest[i * away_count : (i + 1) * away_count] for i in range(4)]
+    rest = rest[6 * away_count :]
+    out, mixed, rest = rest[0], rest[1 : 1 + 2 * away_count], rest[1 + 2 * away_count :]
+    planes, e_high, e_low, spread, staged, sems = rest
     kinds, _, rows, width = mine.shape
     row_count = cores * rows
-    operators = mixed[0].shape[0]
+    operators = near_high.shape[0]
     sinks = out.shape[3]
     lanes = out.shape[5]
     depth_rows = width // chips
 
+    for index in range(away_count):
+        spread_out((late[index], late_other[index]), spread.at[index])
+
+    def mix_late(operator):
+        for index in range(away_count):
+            mix_one(steps, where, gamma, pattern, operator, spread.at[index], mixed[2 * index], mixed[2 * index + 1])
+
+    mix_late(0)
     for away in range(chips):
         plane = where[2] ^ away
         for kind in range(kinds):
@@ -286,10 +305,16 @@
                     part = piece[:, away * depth_rows : (away + 1) * depth_rows]
                     for row, col, sign in spots:
                         scratch[operator, away, row : row + row_count, col : col + depth_rows] = part if sign > 0 else -part
+        if operator + 1 < operators:
+            mix_late(operator + 1)
         result = None
         for away in range(chips):
             left = (e_high[operator, away], e_low[operator, away])
-            right = (mixed[2 * away][operator], mixed[2 * away + 1][operator])
+            if away == 0:
+                right = (near_high, near_low)
+            else:
+                right = mixed[2 * away - 2 : 2 * away]
+            right = [flat(value[operator]) for value in right]
             term = three_pass(left, right, ((1,), (1,)))
             result = term if result is None else result + term
         for part in range(2):
@@ -306,34 +331,39 @@
         copy.wait()
 
 
-def products(where, directions, momenta, mine, theirs, far, far_other, mixed, shape, chips, cores):
-    kinds, width = mine.shape[0], mine.shape[3]
-    rows = cores * mine.shape[2]
+def products(where, scalars, mine, theirs, near, far, far_other, late, late_other, mixed, steps, shape, chips, cores):
+    kinds, _, rows, width = mine.shape
+    spins = scalars[0].shape[2]
+    cols, depth_rows = late[0].shape[3:]
+    left = pltpu.VMEM((shape[1], chips, 2 * cores * rows, 2 * depth_rows), bf16)
     tables = [
         [float(v) for v in fn(np.arange(chips, dtype=np.float32) * np.float32(2.0 * math.pi / chips))]
         for fn in (np.cos, np.sin)
     ]
-    operands = [where, directions, momenta, mine, theirs, *far, *far_other, *mixed]
+    operands = [where, *scalars, mine, theirs, *near, *far, *far_other, *late, *late_other, *mixed]
+    outs = [jax.ShapeDtypeStruct(shape, f32)] + [jax.ShapeDtypeStruct(v.shape, v.dtype) for v in mixed]
     return pl.pallas_call(
-        functools.partial(products_body, chips, cores, tables),
-        out_shape=jax.ShapeDtypeStruct(shape, f32),
-        in_specs=[SMEM] * 3 + [VMEM] * (len(operands) - 3),
-        out_specs=HBM,
+        functools.partial(products_body, chips, cores, steps, tables),
+        out_shape=outs,
+        in_specs=[SMEM] * 5 + [VMEM] * (len(operands) - 5),
+        out_specs=[HBM] + [VMEM] * len(mixed),
+        input_output_aliases={len(operands) - len(mixed) + i: 1 + i for i in range(len(mixed))},
         scratch_shapes=[
-            pltpu.VMEM((chips, kinds, 2, rows, width), f32),
-            pltpu.VMEM((shape[1], chips, 2 * rows, 2 * width // chips), bf16),
-            pltpu.VMEM((shape[1], chips, 2 * rows, 2 * width // chips), bf16),
+            pltpu.VMEM((chips, kinds, 2, cores * rows, width), f32),
+            left,
+            left,
+            pltpu.VMEM((chips - 1, len(steps), 3, spins, cols, depth_rows), f32),
             pltpu.VMEM((shape[1], 2) + shape[3:], f32),
             pltpu.SemaphoreType.DMA((shape[1],)),
         ],
         name="products",
         cost_estimate=pl.CostEstimate(
-            flops=3 * 2 * shape[1] * shape[3] * 2 * rows * 2 * width * shape[5],
+            flops=3 * 2 * shape[1] * shape[3] * 2 * shape[4] * 2 * width * shape[5],
             bytes_accessed=4 * math.prod(shape),
             transcendentals=0,
         ),
         compiler_params=pltpu.CompilerParams(vmem_limit_bytes=24 << 20),
-    )(*operands)
+    )(*operands)[0]
 
 
 def program(eigenvectors, displaced, perambulators, gamma_values, spin_pattern, directions, momenta):
@@ -365,16 +395,22 @@
     for d in later:
         gathered[d] = [partner(early[d], "space", away) for away in range(1, chips)]
     gathered[0] = [value[0] for value in crossed]
-    mixed = []
-    for away in range(chips):
-        if away == 0:
-            here = jnp.stack([blocks[0]] + [early[d] for d in range(1, times)])
-        else:
-            here = jnp.stack([gathered[d][away - 1] for d in range(times)])
+    here = jnp.stack([blocks[0]] + [early[d] for d in range(1, times)])
+    there = partner(here, "spin", 1)
+    mixing = functools.partial(mix, where, gamma_values, spin_pattern)
+    near = mixing(here, there, tuple(range(times)), times, cores)
+    mixed, late, late_other = [], [], []
+    for away in range(chips - 1):
+        here = jnp.stack([gathered[d][away] for d in first])
         there = partner(here, "spin", 1)
-        mixed += mix(where, gamma_values, spin_pattern, here, there, cores)
+        mixed += mixing(here, there, tuple(first), times, cores)
+        late.append(jnp.stack([gathered[d][away] for d in later]))
+        late_other.append(partner(late[-1], "spin", 1))
+    scalars = [gamma_values, spin_pattern, directions, momenta]
     shape = (2, operators, eigenvectors.shape[1], spins // cores, width // chips, perambulators.shape[4] * times)
-    return products(where, directions, momenta, own, theirs, far, far_other, mixed, shape, chips, cores)
+    return products(
+        where, scalars, own, theirs, near, far, far_other, late, late_other, mixed, tuple(later), shape, chips, cores
+    )
 
 
 def solution(mesh):

time: 43.1 us -> 41.4 us (0.961)
  waiting for transfers between devices: 14 us -> 11.6 us
    ppermute x14 -> x15, waiting for transfers between devices: 14 us -> 11.6 us  [partner(): return lax.ppermute(value, axis, [(i, i ^ distance) for i in range(size)])]
    ppermute x14 -> x15, starting transfers between devices: 14 us -> 14.3 us  [partner(): return lax.ppermute(value, axis, [(i, i ^ distance) for i in range(size)])]
  transfers between devices with their start and end apart: 14 -> 15, of which waited for: 3 -> 5; matrix products, arithmetic and copies ran while one was open for 0% -> 0% of each run, Pallas kernels for 26% -> 26%
where the time goes in v3:
time: 41.4 us; the launch traced here: 41.2 us
  Pallas kernels  14.9 us (36%)
  starting transfers between devices  14.3 us (35%)
  waiting for transfers between devices  11.6 us (28%)
    ppermute x15, starting transfers between devices, partner(): return lax.ppermute(value, axis, [(i, i ^ distance) for i in range(size)])  14.3 us
    ppermute x15, waiting for transfers between devices, partner(): return lax.ppermute(value, axis, [(i, i ^ distance) for i in range(size)])  11.6 us
    pallas_call x1, Pallas kernels, sums(): pl.pallas_call(functools.partial(sums_body, chips, cores), out_shape=[own...  4.86 us
    pallas_call x2, Pallas kernels, mix(): pl.pallas_call(functools.partial(mix_body, steps), out_shape=[out, out],...  4.36 us
    pallas_call x1, Pallas kernels, products(): pl.pallas_call(functools.partial(products_body, chips, cores, steps, tabl...  4.01 us
    pallas_call x1, Pallas kernels, pack(): pl.pallas_call(functools.partial(pack_body, first), out_shape=[jax.ShapeD...  1.65 us
  transfers between devices with their start and end apart: 15, of which 5 were waited for; matrix products, arithmetic and copies ran while one was open for 0% of the time, Pallas kernels for 26%

profile of v3, /device:TPU:0, one launch (start us, length us, event | category | flops | bytes accessed | tf_op | source)
XLA Modules:
  0.0 41.2 jit_solution(633798466858932207)
XLA Ops:
  0.0 0.5 %collective-permute-start.1 = (f32[2,3,1,3,128,256]{5,4,3,2,1,0:T(8,128)}, f32[2,3,1,3,128,256]{5,4,3,2,1,0:T(8,128)S(1)}, u32[]{:S(2)}, u32[]{:S(2)}) collective-permute-start(f32[2,3,1,3,128,256]{5,4,3,2,1,0:T(8,128)} %moved.1), channel_id=1, source_target_pairs={{0,1},{1,0},{2,3},{3,2},{4,5},{5,4},{6,7},{7,6},{8,9},{9,8},{10,11... | collective-permute-start | bytes 7077896 | tf_op jit(solution)/shard_map/ppermute | solution.py:43
  0.5 0.0 collective-permute-start
  0.5 0.1 pad_add_fusion.where
  0.6 1.7 %pack.1 = (f32[3,2,2,64,128]{4,3,2,1,0:T(8,128)S(1)}, f32[2,2,64,128]{3,2,1,0:T(8,128)S(1)}, f32[2,2,64,128]{3,2,1,0:T(8,128)S(1)}, f32[2,2,64,128]{3,2,1,0:T(8,128)S(1)}, f32[2,2,64,128]{3,2,1,0:T(8,128)S(1)}) custom-call(s32[4]{0:T(128)S(1)} %pad_add_fusion.where, f32[2,4,2,64,128]{4,3,2,1,0:T(8,128)} %bitcast.21), custom_call_target="tpu_custom_call" | custom-call | bytes 1572864 | tf_op jit(solution)/shard_map/pack/pallas_call | solution.py:62
  2.2 3.0 %collective-permute-start.11 = (f32[3,2,2,64,128]{4,3,2,1,0:T(8,128)S(1)}, f32[3,2,2,64,128]{4,3,2,1,0:T(8,128)S(1)}, u32[]{:S(2)}, u32[]{:S(2)}) collective-permute-start(f32[3,2,2,64,128]{4,3,2,1,0:T(8,128)S(1)} %get-tuple-element.25), channel_id=1, source_target_pairs={{0,2},{2,0},{1,3},{3,1},{4,6},{6,4},{5,7},{7,5},{8,10},{10,8},{9,1... | collective-permute-start | bytes 1179656 | tf_op jit(solution)/shard_map/ppermute | solution.py:43
  5.3 1.6 %collective-permute-start.3 = (f32[2,2,64,128]{3,2,1,0:T(8,128)S(1)}, f32[2,2,64,128]{3,2,1,0:T(8,128)S(1)}, u32[]{:S(2)}, u32[]{:S(2)}) collective-permute-start(f32[2,2,64,128]{3,2,1,0:T(8,128)S(1)} %get-tuple-element.19), channel_id=1, source_target_pairs={{0,4},{4,0},{8,12},{12,8},{1,5},{5,1},{9,13},{13,9},{2,6},{6,2},{1... | collective-permute-start | bytes 393224 | tf_op jit(solution)/shard_map/ppermute | solution.py:43
  6.9 2.6 %collective-permute-start.4 = (f32[2,2,64,128]{3,2,1,0:T(8,128)S(1)}, f32[2,2,64,128]{3,2,1,0:T(8,128)S(1)}, u32[]{:S(2)}, u32[]{:S(2)}) collective-permute-start(f32[2,2,64,128]{3,2,1,0:T(8,128)S(1)} %get-tuple-element.20), channel_id=1, source_target_pairs={{0,8},{4,12},{8,0},{12,4},{1,9},{5,13},{9,1},{13,5},{2,10},{6,14},... | collective-permute-start | bytes 393224 | tf_op jit(solution)/shard_map/ppermute | solution.py:43
  9.4 1.5 %collective-permute-start.5 = (f32[2,2,64,128]{3,2,1,0:T(8,128)S(1)}, f32[2,2,64,128]{3,2,1,0:T(8,128)S(1)}, u32[]{:S(2)}, u32[]{:S(2)}) collective-permute-start(f32[2,2,64,128]{3,2,1,0:T(8,128)S(1)} %get-tuple-element.21), channel_id=1, source_target_pairs={{0,12},{4,8},{8,4},{12,0},{1,13},{5,9},{9,5},{13,1},{2,14},{6,10},... | collective-permute-start | bytes 393224 | tf_op jit(solution)/shard_map/ppermute | solution.py:43
  11.0 4.9 %sums.1 = (f32[3,2,64,256]{3,2,1,0:T(8,128)S(1)}, f32[3,1,2,64,256]{4,3,2,1,0:T(8,128)S(1)}) custom-call(s32[4]{0:T(128)S(1)} %pad_add_fusion.where, f32[2,1,3,128,256]{4,3,2,1,0:T(8,128)} %vectors.1, f32[2,3,1,3,128,256]{5,4,3,2,1,0:T(8,128)} %moved.1, f32[2,1,3,128,256]{4,3,2,1,0:T(8,128)S(1)} %collective-permute-done.v_other, ...), custom_call_target="tpu_custom_call" | custom-call | flops 1811939328 | bytes 6291456 | tf_op jit(solution)/shard_map/sums/pallas_call | solution.py:137
  15.8 0.0 copy-start.2
  15.9 1.6 %collective-permute-start.7 = (f32[3,2,64,256]{3,2,1,0:T(8,128)S(1)}, f32[3,2,64,256]{3,2,1,0:T(8,128)S(1)}, u32[]{:S(2)}, u32[]{:S(2)}) collective-permute-start(f32[3,2,64,256]{3,2,1,0:T(8,128)S(1)} %bitcast.20), channel_id=1, source_target_pairs={{0,2},{2,0},{1,3},{3,1},{4,6},{6,4},{5,7},{7,5},{8,10},{10,8},{9,1... | collective-permute-start | bytes 1179656 | tf_op jit(solution)/shard_map/ppermute | solution.py:43
  17.5 1.4 %collective-permute-start.13 = (f32[2,2,64,128]{3,2,1,0:T(8,128)S(1)}, f32[2,2,64,128]{3,2,1,0:T(8,128)S(1)}, u32[]{:S(2)}, u32[]{:S(2)}) collective-permute-start(f32[2,2,64,128]{3,2,1,0:T(8,128)S(1)} %get-tuple-element.30), channel_id=1, source_target_pairs={{0,12},{4,8},{8,4},{12,0},{1,13},{5,9},{9,5},{13,1},{2,14},{6,10},... | collective-permute-start | bytes 393224 | tf_op jit(solution)/shard_map/ppermute | solution.py:43
  18.9 0.8 %collective-permute-done.4 = f32[2,2,64,128]{3,2,1,0:T(8,128)S(1)} collective-permute-done((f32[2,2,64,128]{3,2,1,0:T(8,128)S(1)}, f32[2,2,64,128]{3,2,1,0:T(8,128)S(1)}, u32[]{:S(2)}, u32[]{:S(2)}) %collective-permute-start.4) | collective-permute-done | bytes 131104 | tf_op jit(solution)/shard_map/ppermute | solution.py:43
  19.7 0.1 collective-permute-start.6
  19.8 5.9 %collective-permute-done.13 = f32[2,2,64,128]{3,2,1,0:T(8,128)S(1)} collective-permute-done((f32[2,2,64,128]{3,2,1,0:T(8,128)S(1)}, f32[2,2,64,128]{3,2,1,0:T(8,128)S(1)}, u32[]{:S(2)}, u32[]{:S(2)}) %collective-permute-start.13) | collective-permute-done | bytes 131104 | tf_op jit(solution)/shard_map/ppermute | solution.py:43
  25.7 0.1 collective-permute-done.12
  25.8 0.1 collective-permute-start.14
  25.9 0.5 %collective-permute-start.2 = (f32[3,2,64,256]{3,2,1,0:T(8,128)S(1)}, f32[3,2,64,256]{3,2,1,0:T(8,128)S(1)}, u32[]{:S(2)}, u32[]{:S(2)}) collective-permute-start(f32[3,2,64,256]{3,2,1,0:T(8,128)S(1)} %get-tuple-element.17.mine), channel_id=1, source_target_pairs={{0,1},{1,0},{2,3},{3,2},{4,5},{5,4},{6,7},{7,6},{8,9},{9,8},{10,11... | collective-permute-start | bytes 1179656 | tf_op jit(solution)/shard_map/ppermute | solution.py:43
  26.4 0.4 collective-permute-done.7.rest_0_
  26.8 1.5 %collective-permute-start.9 = (f32[2,2,64,128]{3,2,1,0:T(8,128)S(1)}, f32[2,2,64,128]{3,2,1,0:T(8,128)S(1)}, u32[]{:S(2)}, u32[]{:S(2)}) collective-permute-start(f32[2,2,64,128]{3,2,1,0:T(8,128)S(1)} %collective-permute-done.4), channel_id=1, source_target_pairs={{0,2},{2,0},{1,3},{3,1},{4,6},{6,4},{5,7},{7,5},{8,10},{10,8},{9,1... | collective-permute-start | bytes 393224 | tf_op jit(solution)/shard_map/ppermute | solution.py:43
  28.3 4.4 %collective-permute-done.9 = f32[2,2,64,128]{3,2,1,0:T(8,128)S(1)} collective-permute-done((f32[2,2,64,128]{3,2,1,0:T(8,128)S(1)}, f32[2,2,64,128]{3,2,1,0:T(8,128)S(1)}, u32[]{:S(2)}, u32[]{:S(2)}) %collective-permute-start.9) | collective-permute-done | bytes 131104 | tf_op jit(solution)/shard_map/ppermute | solution.py:43
  32.7 2.3 %mix.2 = (bf16[4,2,256,256]{3,2,1,0:T(8,128)(2,1)S(1)}, bf16[4,2,256,256]{3,2,1,0:T(8,128)(2,1)S(1)}) custom-call(s32[4]{0:T(128)S(1)} %pad_add_fusion.where, f32[2,4,4,4]{3,2,1,0:T(4,128)S(1)} %copy-done, s32[4,4,4]{2,1,0:T(4,128)S(1)} %copy-done.1, f32[4,2,2,64,128]{4,3,2,1,0:T(8,128)S(1)} %pad_maximum_fusion.mine, ...), custom_call_target="tpu_custom_call" | custom-call | flops 8388608 | bytes 2097152 | tf_op jit(solution)/shard_map/mix/pallas_call | solution.py:214
  35.1 2.1 %mix.3 = (bf16[4,2,256,256]{3,2,1,0:T(8,128)(2,1)S(1)}, bf16[4,2,256,256]{3,2,1,0:T(8,128)(2,1)S(1)}) custom-call(s32[4]{0:T(128)S(1)} %pad_add_fusion.where, f32[2,4,4,4]{3,2,1,0:T(4,128)S(1)} %copy-done, s32[4,4,4]{2,1,0:T(4,128)S(1)} %copy-done.1, f32[3,2,2,64,128]{4,3,2,1,0:T(8,128)S(1)} %pad_maximum_fusion.1.mine, ...), custom_call_target="tpu_custom_call" | custom-call | flops 6291456 | bytes 2097152 | tf_op jit(solution)/shard_map/mix/pallas_call | solution.py:214
  37.2 4.0 %products.1 = (f32[2,4,1,2,128,256]{5,4,3,2,1,0:T(8,128)}, bf16[4,2,256,256]{3,2,1,0:T(8,128)(2,1)S(1)}, bf16[4,2,256,256]{3,2,1,0:T(8,128)(2,1)S(1)}) custom-call(s32[4]{0:T(128)S(1)} %pad_add_fusion.where, f32[2,4,4,4]{3,2,1,0:T(4,128)S(1)} %copy-done, s32[4,4,4]{2,1,0:T(4,128)S(1)} %copy-done.1, ...), custom_call_target="tpu_custom_call", output_to_operand_aliasing={{1}: (13, {}), {2}: (14, {})} | custom-call | flops 1610612736 | bytes 2097152 | tf_op jit(solution)/shard_map/products/pallas_call | solution.py:345
  (23 shorter events, 0.2 us)
Async XLA Ops:
  0.0 11.0 %collective-permute-start.1 = (f32[2,3,1,3,128,256]{5,4,3,2,1,0:T(8,128)}, f32[2,3,1,3,128,256]{5,4,3,2,1,0:T(8,128)S(1)}, u32[]{:S(2)}, u32[]{:S(2)}) collective-permute-start(f32[2,3,1,3,128,256]{5,4,3,2,1,0:T(8,128)} %moved.1), channel_id=1, source_target_pairs={{0,1},{1,0},{2,3},{3,2},{4,5},{5,4},{6,7},{7,6},{8,9},{9,8},{10,11... | collective-permute-start | bytes 7077896 | tf_op jit(solution)/shard_map/ppermute | solution.py:43
  0.5 9.0 %collective-permute-start = (f32[2,1,3,128,256]{4,3,2,1,0:T(8,128)}, f32[2,1,3,128,256]{4,3,2,1,0:T(8,128)S(1)}, u32[]{:S(2)}, u32[]{:S(2)}) collective-permute-start(f32[2,1,3,128,256]{4,3,2,1,0:T(8,128)} %vectors.1), channel_id=1, source_target_pairs={{0,1},{1,0},{2,3},{3,2},{4,5},{5,4},{6,7},{7,6},{8,9},{9,8},{10,11... | collective-permute-start | bytes 2359304 | tf_op jit(solution)/shard_map/ppermute | solution.py:43
  2.2 15.2 %collective-permute-start.11 = (f32[3,2,2,64,128]{4,3,2,1,0:T(8,128)S(1)}, f32[3,2,2,64,128]{4,3,2,1,0:T(8,128)S(1)}, u32[]{:S(2)}, u32[]{:S(2)}) collective-permute-start(f32[3,2,2,64,128]{4,3,2,1,0:T(8,128)S(1)} %get-tuple-element.25), channel_id=1, source_target_pairs={{0,2},{2,0},{1,3},{3,1},{4,6},{6,4},{5,7},{7,5},{8,10},{10,8},{9,1... | collective-permute-start | bytes 1179656 | tf_op jit(solution)/shard_map/ppermute | solution.py:43
  5.3 13.6 %collective-permute-start.3 = (f32[2,2,64,128]{3,2,1,0:T(8,128)S(1)}, f32[2,2,64,128]{3,2,1,0:T(8,128)S(1)}, u32[]{:S(2)}, u32[]{:S(2)}) collective-permute-start(f32[2,2,64,128]{3,2,1,0:T(8,128)S(1)} %get-tuple-element.19), channel_id=1, source_target_pairs={{0,4},{4,0},{8,12},{12,8},{1,5},{5,1},{9,13},{13,9},{2,6},{6,2},{1... | collective-permute-start | bytes 393224 | tf_op jit(solution)/shard_map/ppermute | solution.py:43
  6.9 12.8 %collective-permute-start.4 = (f32[2,2,64,128]{3,2,1,0:T(8,128)S(1)}, f32[2,2,64,128]{3,2,1,0:T(8,128)S(1)}, u32[]{:S(2)}, u32[]{:S(2)}) collective-permute-start(f32[2,2,64,128]{3,2,1,0:T(8,128)S(1)} %get-tuple-element.20), channel_id=1, source_target_pairs={{0,8},{4,12},{8,0},{12,4},{1,9},{5,13},{9,1},{13,5},{2,10},{6,14},... | collective-permute-start | bytes 393224 | tf_op jit(solution)/shard_map/ppermute | solution.py:43
  9.4 10.2 %collective-permute-start.5 = (f32[2,2,64,128]{3,2,1,0:T(8,128)S(1)}, f32[2,2,64,128]{3,2,1,0:T(8,128)S(1)}, u32[]{:S(2)}, u32[]{:S(2)}) collective-permute-start(f32[2,2,64,128]{3,2,1,0:T(8,128)S(1)} %get-tuple-element.21), channel_id=1, source_target_pairs={{0,12},{4,8},{8,4},{12,0},{1,13},{5,9},{9,5},{13,1},{2,14},{6,10},... | collective-permute-start | bytes 393224 | tf_op jit(solution)/shard_map/ppermute | solution.py:43
  15.8 16.9 %copy-start = (f32[2,4,4,4]{3,2,1,0:T(4,128)S(1)}, f32[2,4,4,4]{3,2,1,0:T(4,128)}, u32[]{:S(2)}) copy-start(f32[2,4,4,4]{3,2,1,0:T(4,128)} %gamma.5) | copy-start | bytes 1540
  15.8 16.9 %copy-start.1 = (s32[4,4,4]{2,1,0:T(4,128)S(1)}, s32[4,4,4]{2,1,0:T(4,128)}, u32[]{:S(2)}) copy-start(s32[4,4,4]{2,1,0:T(4,128)} %pattern.5) | copy-start | bytes 772
  15.8 21.3 %copy-start.2 = (s32[4]{0:T(128)S(1)}, s32[4]{0:T(128)}, u32[]{:S(2)}) copy-start(s32[4]{0:T(128)} %directions.1) | copy-start | bytes 52
  15.9 21.3 %copy-start.3 = (s32[4]{0:T(128)S(1)}, s32[4]{0:T(128)}, u32[]{:S(2)}) copy-start(s32[4]{0:T(128)} %momenta.1) | copy-start | bytes 52
  15.9 10.9 %collective-permute-start.7 = (f32[3,2,64,256]{3,2,1,0:T(8,128)S(1)}, f32[3,2,64,256]{3,2,1,0:T(8,128)S(1)}, u32[]{:S(2)}, u32[]{:S(2)}) collective-permute-start(f32[3,2,64,256]{3,2,1,0:T(8,128)S(1)} %bitcast.20), channel_id=1, source_target_pairs={{0,2},{2,0},{1,3},{3,1},{4,6},{6,4},{5,7},{7,5},{8,10},{10,8},{9,1... | collective-permute-start | bytes 1179656 | tf_op jit(solution)/shard_map/ppermute | solution.py:43
  17.5 8.2 %collective-permute-start.13 = (f32[2,2,64,128]{3,2,1,0:T(8,128)S(1)}, f32[2,2,64,128]{3,2,1,0:T(8,128)S(1)}, u32[]{:S(2)}, u32[]{:S(2)}) collective-permute-start(f32[2,2,64,128]{3,2,1,0:T(8,128)S(1)} %get-tuple-element.30), channel_id=1, source_target_pairs={{0,12},{4,8},{8,4},{12,0},{1,13},{5,9},{9,5},{13,1},{2,14},{6,10},... | collective-permute-start | bytes 393224 | tf_op jit(solution)/shard_map/ppermute | solution.py:43
  18.9 6.9 %collective-permute-start.12 = (f32[2,2,64,128]{3,2,1,0:T(8,128)S(1)}, f32[2,2,64,128]{3,2,1,0:T(8,128)S(1)}, u32[]{:S(2)}, u32[]{:S(2)}) collective-permute-start(f32[2,2,64,128]{3,2,1,0:T(8,128)S(1)} %get-tuple-element.31), channel_id=1, source_target_pairs={{0,4},{4,0},{8,12},{12,8},{1,5},{5,1},{9,13},{13,9},{2,6},{6,2},{1... | collective-permute-start | bytes 393224 | tf_op jit(solution)/shard_map/ppermute | solution.py:43
  19.7 13.0 %collective-permute-start.6 = (f32[4,2,2,64,128]{4,3,2,1,0:T(8,128)S(1)}, f32[4,2,2,64,128]{4,3,2,1,0:T(8,128)S(1)}, u32[]{:S(2)}, u32[]{:S(2)}) collective-permute-start(f32[4,2,2,64,128]{4,3,2,1,0:T(8,128)S(1)} %pad_maximum_fusion.mine), channel_id=1, source_target_pairs={{0,1},{1,0},{2,3},{3,2},{4,5},{5,4},{6,7},{7,6},{8,9},{9,8},{10,11... | collective-permute-start | bytes 1572872 | tf_op jit(solution)/shard_map/ppermute | solution.py:43
  25.8 9.2 %collective-permute-start.14 = (f32[3,2,2,64,128]{4,3,2,1,0:T(8,128)S(1)}, f32[3,2,2,64,128]{4,3,2,1,0:T(8,128)S(1)}, u32[]{:S(2)}, u32[]{:S(2)}) collective-permute-start(f32[3,2,2,64,128]{4,3,2,1,0:T(8,128)S(1)} %pad_maximum_fusion.1.mine), channel_id=1, source_target_pairs={{0,1},{1,0},{2,3},{3,2},{4,5},{5,4},{6,7},{7,6},{8,9},{9,8},{10,11... | collective-permute-start | bytes 1179656 | tf_op jit(solution)/shard_map/ppermute | solution.py:43
  25.9 11.2 %collective-permute-start.2 = (f32[3,2,64,256]{3,2,1,0:T(8,128)S(1)}, f32[3,2,64,256]{3,2,1,0:T(8,128)S(1)}, u32[]{:S(2)}, u32[]{:S(2)}) collective-permute-start(f32[3,2,64,256]{3,2,1,0:T(8,128)S(1)} %get-tuple-element.17.mine), channel_id=1, source_target_pairs={{0,1},{1,0},{2,3},{3,2},{4,5},{5,4},{6,7},{7,6},{8,9},{9,8},{10,11... | collective-permute-start | bytes 1179656 | tf_op jit(solution)/shard_map/ppermute | solution.py:43
  26.8 10.3 %collective-permute-start.8 = (f32[3,2,64,256]{3,2,1,0:T(8,128)S(1)}, f32[3,2,64,256]{3,2,1,0:T(8,128)S(1)}, u32[]{:S(2)}, u32[]{:S(2)}) collective-permute-start(f32[3,2,64,256]{3,2,1,0:T(8,128)S(1)} %collective-permute-done.7.rest_0_), channel_id=1, source_target_pairs={{0,1},{1,0},{2,3},{3,2},{4,5},{5,4},{6,7},{7,6},{8,9},{9,8},{10,11... | collective-permute-start | bytes 1179656 | tf_op jit(solution)/shard_map/ppermute | solution.py:43
  26.8 5.9 %collective-permute-start.9 = (f32[2,2,64,128]{3,2,1,0:T(8,128)S(1)}, f32[2,2,64,128]{3,2,1,0:T(8,128)S(1)}, u32[]{:S(2)}, u32[]{:S(2)}) collective-permute-start(f32[2,2,64,128]{3,2,1,0:T(8,128)S(1)} %collective-permute-done.4), channel_id=1, source_target_pairs={{0,2},{2,0},{1,3},{3,1},{4,6},{6,4},{5,7},{7,5},{8,10},{10,8},{9,1... | collective-permute-start | bytes 393224 | tf_op jit(solution)/shard_map/ppermute | solution.py:43
  32.7 4.4 %collective-permute-start.10 = (f32[1,2,2,64,128]{4,3,2,1,0:T(8,128)S(1)}, f32[1,2,2,64,128]{4,3,2,1,0:T(8,128)S(1)}, u32[]{:S(2)}, u32[]{:S(2)}) collective-permute-start(f32[1,2,2,64,128]{4,3,2,1,0:T(8,128)S(1)} %bitcast.18), channel_id=1, source_target_pairs={{0,1},{1,0},{2,3},{3,2},{4,5},{5,4},{6,7},{7,6},{8,9},{9,8},{10,11... | collective-permute-start | bytes 393224 | tf_op jit(solution)/shard_map/ppermute | solution.py:43

commit v4 on v3

--- a/solution.py
+++ b/solution.py
@@ -44,16 +44,18 @@
 
 
 def pack_body(first, where, peram, together, *rest):
-    outs, buffer, sem = rest[:-2], rest[-2], rest[-1]
-    copy = pltpu.make_async_copy(peram, buffer, sem)
-    copy.start()
-    copy.wait()
+    outs, buffer, sems = rest[:-2], rest[-2], rest[-1]
+    copies = [
+        pltpu.make_async_copy(peram.at[:, where[1] ^ distance], buffer.at[distance], sems.at[distance])
+        for distance in range(len(outs))
+    ]
+    for copy in copies:
+        copy.start()
     for distance, out in enumerate(outs):
-        for part in range(buffer.shape[0]):
-            block = buffer[part, where[1] ^ distance]
-            out[part] = block
-            if distance in first:
-                together[first.index(distance), part] = block
+        copies[distance].wait()
+        out[...] = buffer[distance]
+        if distance in first:
+            together[first.index(distance)] = buffer[distance]
 
 
 def pack(where, peram, first):
@@ -64,7 +66,7 @@
         out_shape=[jax.ShapeDtypeStruct(dims, f32) for dims in [(len(first),) + one] + [one] * times],
         in_specs=[SMEM, HBM],
         out_specs=[VMEM] * (times + 1),
-        scratch_shapes=[pltpu.VMEM(peram.shape, f32), pltpu.SemaphoreType.DMA],
+        scratch_shapes=[pltpu.VMEM((times,) + one, f32), pltpu.SemaphoreType.DMA((times,))],
         name="pack",
         cost_estimate=pl.CostEstimate(flops=0, bytes_accessed=peram.size * 12, transcendentals=0),
         compiler_params=pltpu.CompilerParams(vmem_limit_bytes=8 << 20),
@@ -325,8 +327,10 @@
                         part * row_count + core * rows : part * row_count + (core + 1) * rows,
                         sink * lanes : (sink + 1) * lanes,
                     ]
-        copies.append(pltpu.make_async_copy(staged.at[operator], out.at[:, operator, 0], sems.at[operator]))
-        copies[-1].start()
+            copies.append(
+                pltpu.make_async_copy(staged.at[operator, part], out.at[part, operator, 0], sems.at[operator, part])
+            )
+            copies[-1].start()
     for copy in copies:
         copy.wait()
 
@@ -354,7 +358,7 @@
             left,
             pltpu.VMEM((chips - 1, len(steps), 3, spins, cols, depth_rows), f32),
             pltpu.VMEM((shape[1], 2) + shape[3:], f32),
-            pltpu.SemaphoreType.DMA((shape[1],)),
+            pltpu.SemaphoreType.DMA((shape[1], 2)),
         ],
         name="products",
         cost_estimate=pl.CostEstimate(

time: 41.4 us -> 41.3 us (level)
  no operation moved by 1% of the time
where the time goes in v4:
time: 41.3 us; the launch traced here: 41.2 us
  Pallas kernels  14.9 us (36%)
  starting transfers between devices  14.3 us (35%)
  waiting for transfers between devices  11.6 us (28%)
    ppermute x15, starting transfers between devices, partner(): return lax.ppermute(value, axis, [(i, i ^ distance) for i in range(size)])  14.3 us
    ppermute x15, waiting for transfers between devices, partner(): return lax.ppermute(value, axis, [(i, i ^ distance) for i in range(size)])  11.6 us
    pallas_call x1, Pallas kernels, sums(): pl.pallas_call(functools.partial(sums_body, chips, cores), out_shape=[own...  4.86 us
    pallas_call x2, Pallas kernels, mix(): pl.pallas_call(functools.partial(mix_body, steps), out_shape=[out, out],...  4.36 us
    pallas_call x1, Pallas kernels, products(): pl.pallas_call(functools.partial(products_body, chips, cores, steps, tabl...  4.01 us
    pallas_call x1, Pallas kernels, pack(): pl.pallas_call(functools.partial(pack_body, first), out_shape=[jax.ShapeD...  1.69 us
  transfers between devices with their start and end apart: 15, of which 5 were waited for; matrix products, arithmetic and copies ran while one was open for 0% of the time, Pallas kernels for 26%

profile of v4, /device:TPU:0, one launch (start us, length us, event | category | flops | bytes accessed | tf_op | source)
XLA Modules:
  0.0 41.2 jit_solution(6563339026716891819)
XLA Ops:
  0.0 0.5 %collective-permute-start.1 = (f32[2,3,1,3,128,256]{5,4,3,2,1,0:T(8,128)}, f32[2,3,1,3,128,256]{5,4,3,2,1,0:T(8,128)S(1)}, u32[]{:S(2)}, u32[]{:S(2)}) collective-permute-start(f32[2,3,1,3,128,256]{5,4,3,2,1,0:T(8,128)} %moved.1), channel_id=1, source_target_pairs={{0,1},{1,0},{2,3},{3,2},{4,5},{5,4},{6,7},{7,6},{8,9},{9,8},{10,11... | collective-permute-start | bytes 7077896 | tf_op jit(solution)/shard_map/ppermute | solution.py:43
  0.5 0.0 collective-permute-start
  0.5 0.1 pad_add_fusion.where
  0.6 1.7 %pack.1 = (f32[3,2,2,64,128]{4,3,2,1,0:T(8,128)S(1)}, f32[2,2,64,128]{3,2,1,0:T(8,128)S(1)}, f32[2,2,64,128]{3,2,1,0:T(8,128)S(1)}, f32[2,2,64,128]{3,2,1,0:T(8,128)S(1)}, f32[2,2,64,128]{3,2,1,0:T(8,128)S(1)}) custom-call(s32[4]{0:T(128)S(1)} %pad_add_fusion.where, f32[2,4,2,64,128]{4,3,2,1,0:T(8,128)} %bitcast.21), custom_call_target="tpu_custom_call" | custom-call | bytes 1572864 | tf_op jit(solution)/shard_map/pack/pallas_call | solution.py:64
  2.3 3.0 %collective-permute-start.11 = (f32[3,2,2,64,128]{4,3,2,1,0:T(8,128)S(1)}, f32[3,2,2,64,128]{4,3,2,1,0:T(8,128)S(1)}, u32[]{:S(2)}, u32[]{:S(2)}) collective-permute-start(f32[3,2,2,64,128]{4,3,2,1,0:T(8,128)S(1)} %get-tuple-element.25), channel_id=1, source_target_pairs={{0,2},{2,0},{1,3},{3,1},{4,6},{6,4},{5,7},{7,5},{8,10},{10,8},{9,1... | collective-permute-start | bytes 1179656 | tf_op jit(solution)/shard_map/ppermute | solution.py:43
  5.3 1.6 %collective-permute-start.3 = (f32[2,2,64,128]{3,2,1,0:T(8,128)S(1)}, f32[2,2,64,128]{3,2,1,0:T(8,128)S(1)}, u32[]{:S(2)}, u32[]{:S(2)}) collective-permute-start(f32[2,2,64,128]{3,2,1,0:T(8,128)S(1)} %get-tuple-element.19), channel_id=1, source_target_pairs={{0,4},{4,0},{8,12},{12,8},{1,5},{5,1},{9,13},{13,9},{2,6},{6,2},{1... | collective-permute-start | bytes 393224 | tf_op jit(solution)/shard_map/ppermute | solution.py:43
  6.9 2.6 %collective-permute-start.4 = (f32[2,2,64,128]{3,2,1,0:T(8,128)S(1)}, f32[2,2,64,128]{3,2,1,0:T(8,128)S(1)}, u32[]{:S(2)}, u32[]{:S(2)}) collective-permute-start(f32[2,2,64,128]{3,2,1,0:T(8,128)S(1)} %get-tuple-element.20), channel_id=1, source_target_pairs={{0,8},{4,12},{8,0},{12,4},{1,9},{5,13},{9,1},{13,5},{2,10},{6,14},... | collective-permute-start | bytes 393224 | tf_op jit(solution)/shard_map/ppermute | solution.py:43
  9.5 1.5 %collective-permute-start.5 = (f32[2,2,64,128]{3,2,1,0:T(8,128)S(1)}, f32[2,2,64,128]{3,2,1,0:T(8,128)S(1)}, u32[]{:S(2)}, u32[]{:S(2)}) collective-permute-start(f32[2,2,64,128]{3,2,1,0:T(8,128)S(1)} %get-tuple-element.21), channel_id=1, source_target_pairs={{0,12},{4,8},{8,4},{12,0},{1,13},{5,9},{9,5},{13,1},{2,14},{6,10},... | collective-permute-start | bytes 393224 | tf_op jit(solution)/shard_map/ppermute | solution.py:43
  11.0 4.9 %sums.1 = (f32[3,2,64,256]{3,2,1,0:T(8,128)S(1)}, f32[3,1,2,64,256]{4,3,2,1,0:T(8,128)S(1)}) custom-call(s32[4]{0:T(128)S(1)} %pad_add_fusion.where, f32[2,1,3,128,256]{4,3,2,1,0:T(8,128)} %vectors.1, f32[2,3,1,3,128,256]{5,4,3,2,1,0:T(8,128)} %moved.1, f32[2,1,3,128,256]{4,3,2,1,0:T(8,128)S(1)} %collective-permute-done.v_other, ...), custom_call_target="tpu_custom_call" | custom-call | flops 1811939328 | bytes 6291456 | tf_op jit(solution)/shard_map/sums/pallas_call | solution.py:139
  15.8 0.0 copy-start.2
  15.9 1.6 %collective-permute-start.7 = (f32[3,2,64,256]{3,2,1,0:T(8,128)S(1)}, f32[3,2,64,256]{3,2,1,0:T(8,128)S(1)}, u32[]{:S(2)}, u32[]{:S(2)}) collective-permute-start(f32[3,2,64,256]{3,2,1,0:T(8,128)S(1)} %bitcast.20), channel_id=1, source_target_pairs={{0,2},{2,0},{1,3},{3,1},{4,6},{6,4},{5,7},{7,5},{8,10},{10,8},{9,1... | collective-permute-start | bytes 1179656 | tf_op jit(solution)/shard_map/ppermute | solution.py:43
  17.5 1.5 %collective-permute-start.13 = (f32[2,2,64,128]{3,2,1,0:T(8,128)S(1)}, f32[2,2,64,128]{3,2,1,0:T(8,128)S(1)}, u32[]{:S(2)}, u32[]{:S(2)}) collective-permute-start(f32[2,2,64,128]{3,2,1,0:T(8,128)S(1)} %get-tuple-element.30), channel_id=1, source_target_pairs={{0,12},{4,8},{8,4},{12,0},{1,13},{5,9},{9,5},{13,1},{2,14},{6,10},... | collective-permute-start | bytes 393224 | tf_op jit(solution)/shard_map/ppermute | solution.py:43
  18.9 0.8 %collective-permute-done.4 = f32[2,2,64,128]{3,2,1,0:T(8,128)S(1)} collective-permute-done((f32[2,2,64,128]{3,2,1,0:T(8,128)S(1)}, f32[2,2,64,128]{3,2,1,0:T(8,128)S(1)}, u32[]{:S(2)}, u32[]{:S(2)}) %collective-permute-start.4) | collective-permute-done | bytes 131104 | tf_op jit(solution)/shard_map/ppermute | solution.py:43
  19.8 0.1 collective-permute-start.6
  19.8 5.8 %collective-permute-done.13 = f32[2,2,64,128]{3,2,1,0:T(8,128)S(1)} collective-permute-done((f32[2,2,64,128]{3,2,1,0:T(8,128)S(1)}, f32[2,2,64,128]{3,2,1,0:T(8,128)S(1)}, u32[]{:S(2)}, u32[]{:S(2)}) %collective-permute-start.13) | collective-permute-done | bytes 131104 | tf_op jit(solution)/shard_map/ppermute | solution.py:43
  25.7 0.1 collective-permute-done.12
  25.8 0.1 collective-permute-start.14
  25.9 0.5 %collective-permute-start.2 = (f32[3,2,64,256]{3,2,1,0:T(8,128)S(1)}, f32[3,2,64,256]{3,2,1,0:T(8,128)S(1)}, u32[]{:S(2)}, u32[]{:S(2)}) collective-permute-start(f32[3,2,64,256]{3,2,1,0:T(8,128)S(1)} %get-tuple-element.17.mine), channel_id=1, source_target_pairs={{0,1},{1,0},{2,3},{3,2},{4,5},{5,4},{6,7},{7,6},{8,9},{9,8},{10,11... | collective-permute-start | bytes 1179656 | tf_op jit(solution)/shard_map/ppermute | solution.py:43
  26.4 0.4 collective-permute-done.7.rest_0_
  26.8 1.5 %collective-permute-start.9 = (f32[2,2,64,128]{3,2,1,0:T(8,128)S(1)}, f32[2,2,64,128]{3,2,1,0:T(8,128)S(1)}, u32[]{:S(2)}, u32[]{:S(2)}) collective-permute-start(f32[2,2,64,128]{3,2,1,0:T(8,128)S(1)} %collective-permute-done.4), channel_id=1, source_target_pairs={{0,2},{2,0},{1,3},{3,1},{4,6},{6,4},{5,7},{7,5},{8,10},{10,8},{9,1... | collective-permute-start | bytes 393224 | tf_op jit(solution)/shard_map/ppermute | solution.py:43
  28.3 4.4 %collective-permute-done.9 = f32[2,2,64,128]{3,2,1,0:T(8,128)S(1)} collective-permute-done((f32[2,2,64,128]{3,2,1,0:T(8,128)S(1)}, f32[2,2,64,128]{3,2,1,0:T(8,128)S(1)}, u32[]{:S(2)}, u32[]{:S(2)}) %collective-permute-start.9) | collective-permute-done | bytes 131104 | tf_op jit(solution)/shard_map/ppermute | solution.py:43
  32.7 2.3 %mix.2 = (bf16[4,2,256,256]{3,2,1,0:T(8,128)(2,1)S(1)}, bf16[4,2,256,256]{3,2,1,0:T(8,128)(2,1)S(1)}) custom-call(s32[4]{0:T(128)S(1)} %pad_add_fusion.where, f32[2,4,4,4]{3,2,1,0:T(4,128)S(1)} %copy-done, s32[4,4,4]{2,1,0:T(4,128)S(1)} %copy-done.1, f32[4,2,2,64,128]{4,3,2,1,0:T(8,128)S(1)} %pad_maximum_fusion.mine, ...), custom_call_target="tpu_custom_call" | custom-call | flops 8388608 | bytes 2097152 | tf_op jit(solution)/shard_map/mix/pallas_call | solution.py:216
  35.1 2.1 %mix.3 = (bf16[4,2,256,256]{3,2,1,0:T(8,128)(2,1)S(1)}, bf16[4,2,256,256]{3,2,1,0:T(8,128)(2,1)S(1)}) custom-call(s32[4]{0:T(128)S(1)} %pad_add_fusion.where, f32[2,4,4,4]{3,2,1,0:T(4,128)S(1)} %copy-done, s32[4,4,4]{2,1,0:T(4,128)S(1)} %copy-done.1, f32[3,2,2,64,128]{4,3,2,1,0:T(8,128)S(1)} %pad_maximum_fusion.1.mine, ...), custom_call_target="tpu_custom_call" | custom-call | flops 6291456 | bytes 2097152 | tf_op jit(solution)/shard_map/mix/pallas_call | solution.py:216
  37.2 4.0 %products.1 = (f32[2,4,1,2,128,256]{5,4,3,2,1,0:T(8,128)}, bf16[4,2,256,256]{3,2,1,0:T(8,128)(2,1)S(1)}, bf16[4,2,256,256]{3,2,1,0:T(8,128)(2,1)S(1)}) custom-call(s32[4]{0:T(128)S(1)} %pad_add_fusion.where, f32[2,4,4,4]{3,2,1,0:T(4,128)S(1)} %copy-done, s32[4,4,4]{2,1,0:T(4,128)S(1)} %copy-done.1, ...), custom_call_target="tpu_custom_call", output_to_operand_aliasing={{1}: (13, {}), {2}: (14, {})} | custom-call | flops 1610612736 | bytes 2097152 | tf_op jit(solution)/shard_map/products/pallas_call | solution.py:349
  (23 shorter events, 0.2 us)
Async XLA Ops:
  0.0 11.0 %collective-permute-start.1 = (f32[2,3,1,3,128,256]{5,4,3,2,1,0:T(8,128)}, f32[2,3,1,3,128,256]{5,4,3,2,1,0:T(8,128)S(1)}, u32[]{:S(2)}, u32[]{:S(2)}) collective-permute-start(f32[2,3,1,3,128,256]{5,4,3,2,1,0:T(8,128)} %moved.1), channel_id=1, source_target_pairs={{0,1},{1,0},{2,3},{3,2},{4,5},{5,4},{6,7},{7,6},{8,9},{9,8},{10,11... | collective-permute-start | bytes 7077896 | tf_op jit(solution)/shard_map/ppermute | solution.py:43
  0.5 9.0 %collective-permute-start = (f32[2,1,3,128,256]{4,3,2,1,0:T(8,128)}, f32[2,1,3,128,256]{4,3,2,1,0:T(8,128)S(1)}, u32[]{:S(2)}, u32[]{:S(2)}) collective-permute-start(f32[2,1,3,128,256]{4,3,2,1,0:T(8,128)} %vectors.1), channel_id=1, source_target_pairs={{0,1},{1,0},{2,3},{3,2},{4,5},{5,4},{6,7},{7,6},{8,9},{9,8},{10,11... | collective-permute-start | bytes 2359304 | tf_op jit(solution)/shard_map/ppermute | solution.py:43
  2.3 15.1 %collective-permute-start.11 = (f32[3,2,2,64,128]{4,3,2,1,0:T(8,128)S(1)}, f32[3,2,2,64,128]{4,3,2,1,0:T(8,128)S(1)}, u32[]{:S(2)}, u32[]{:S(2)}) collective-permute-start(f32[3,2,2,64,128]{4,3,2,1,0:T(8,128)S(1)} %get-tuple-element.25), channel_id=1, source_target_pairs={{0,2},{2,0},{1,3},{3,1},{4,6},{6,4},{5,7},{7,5},{8,10},{10,8},{9,1... | collective-permute-start | bytes 1179656 | tf_op jit(solution)/shard_map/ppermute | solution.py:43
  5.3 13.6 %collective-permute-start.3 = (f32[2,2,64,128]{3,2,1,0:T(8,128)S(1)}, f32[2,2,64,128]{3,2,1,0:T(8,128)S(1)}, u32[]{:S(2)}, u32[]{:S(2)}) collective-permute-start(f32[2,2,64,128]{3,2,1,0:T(8,128)S(1)} %get-tuple-element.19), channel_id=1, source_target_pairs={{0,4},{4,0},{8,12},{12,8},{1,5},{5,1},{9,13},{13,9},{2,6},{6,2},{1... | collective-permute-start | bytes 393224 | tf_op jit(solution)/shard_map/ppermute | solution.py:43
  6.9 12.8 %collective-permute-start.4 = (f32[2,2,64,128]{3,2,1,0:T(8,128)S(1)}, f32[2,2,64,128]{3,2,1,0:T(8,128)S(1)}, u32[]{:S(2)}, u32[]{:S(2)}) collective-permute-start(f32[2,2,64,128]{3,2,1,0:T(8,128)S(1)} %get-tuple-element.20), channel_id=1, source_target_pairs={{0,8},{4,12},{8,0},{12,4},{1,9},{5,13},{9,1},{13,5},{2,10},{6,14},... | collective-permute-start | bytes 393224 | tf_op jit(solution)/shard_map/ppermute | solution.py:43
  9.5 10.2 %collective-permute-start.5 = (f32[2,2,64,128]{3,2,1,0:T(8,128)S(1)}, f32[2,2,64,128]{3,2,1,0:T(8,128)S(1)}, u32[]{:S(2)}, u32[]{:S(2)}) collective-permute-start(f32[2,2,64,128]{3,2,1,0:T(8,128)S(1)} %get-tuple-element.21), channel_id=1, source_target_pairs={{0,12},{4,8},{8,4},{12,0},{1,13},{5,9},{9,5},{13,1},{2,14},{6,10},... | collective-permute-start | bytes 393224 | tf_op jit(solution)/shard_map/ppermute | solution.py:43
  15.8 16.9 %copy-start = (f32[2,4,4,4]{3,2,1,0:T(4,128)S(1)}, f32[2,4,4,4]{3,2,1,0:T(4,128)}, u32[]{:S(2)}) copy-start(f32[2,4,4,4]{3,2,1,0:T(4,128)} %gamma.5) | copy-start | bytes 1540
  15.8 16.9 %copy-start.1 = (s32[4,4,4]{2,1,0:T(4,128)S(1)}, s32[4,4,4]{2,1,0:T(4,128)}, u32[]{:S(2)}) copy-start(s32[4,4,4]{2,1,0:T(4,128)} %pattern.5) | copy-start | bytes 772
  15.8 21.3 %copy-start.2 = (s32[4]{0:T(128)S(1)}, s32[4]{0:T(128)}, u32[]{:S(2)}) copy-start(s32[4]{0:T(128)} %directions.1) | copy-start | bytes 52
  15.9 21.3 %copy-start.3 = (s32[4]{0:T(128)S(1)}, s32[4]{0:T(128)}, u32[]{:S(2)}) copy-start(s32[4]{0:T(128)} %momenta.1) | copy-start | bytes 52
  15.9 10.9 %collective-permute-start.7 = (f32[3,2,64,256]{3,2,1,0:T(8,128)S(1)}, f32[3,2,64,256]{3,2,1,0:T(8,128)S(1)}, u32[]{:S(2)}, u32[]{:S(2)}) collective-permute-start(f32[3,2,64,256]{3,2,1,0:T(8,128)S(1)} %bitcast.20), channel_id=1, source_target_pairs={{0,2},{2,0},{1,3},{3,1},{4,6},{6,4},{5,7},{7,5},{8,10},{10,8},{9,1... | collective-permute-start | bytes 1179656 | tf_op jit(solution)/shard_map/ppermute | solution.py:43
  17.5 8.2 %collective-permute-start.13 = (f32[2,2,64,128]{3,2,1,0:T(8,128)S(1)}, f32[2,2,64,128]{3,2,1,0:T(8,128)S(1)}, u32[]{:S(2)}, u32[]{:S(2)}) collective-permute-start(f32[2,2,64,128]{3,2,1,0:T(8,128)S(1)} %get-tuple-element.30), channel_id=1, source_target_pairs={{0,12},{4,8},{8,4},{12,0},{1,13},{5,9},{9,5},{13,1},{2,14},{6,10},... | collective-permute-start | bytes 393224 | tf_op jit(solution)/shard_map/ppermute | solution.py:43
  18.9 6.9 %collective-permute-start.12 = (f32[2,2,64,128]{3,2,1,0:T(8,128)S(1)}, f32[2,2,64,128]{3,2,1,0:T(8,128)S(1)}, u32[]{:S(2)}, u32[]{:S(2)}) collective-permute-start(f32[2,2,64,128]{3,2,1,0:T(8,128)S(1)} %get-tuple-element.31), channel_id=1, source_target_pairs={{0,4},{4,0},{8,12},{12,8},{1,5},{5,1},{9,13},{13,9},{2,6},{6,2},{1... | collective-permute-start | bytes 393224 | tf_op jit(solution)/shard_map/ppermute | solution.py:43
  19.8 13.0 %collective-permute-start.6 = (f32[4,2,2,64,128]{4,3,2,1,0:T(8,128)S(1)}, f32[4,2,2,64,128]{4,3,2,1,0:T(8,128)S(1)}, u32[]{:S(2)}, u32[]{:S(2)}) collective-permute-start(f32[4,2,2,64,128]{4,3,2,1,0:T(8,128)S(1)} %pad_maximum_fusion.mine), channel_id=1, source_target_pairs={{0,1},{1,0},{2,3},{3,2},{4,5},{5,4},{6,7},{7,6},{8,9},{9,8},{10,11... | collective-permute-start | bytes 1572872 | tf_op jit(solution)/shard_map/ppermute | solution.py:43
  25.8 9.2 %collective-permute-start.14 = (f32[3,2,2,64,128]{4,3,2,1,0:T(8,128)S(1)}, f32[3,2,2,64,128]{4,3,2,1,0:T(8,128)S(1)}, u32[]{:S(2)}, u32[]{:S(2)}) collective-permute-start(f32[3,2,2,64,128]{4,3,2,1,0:T(8,128)S(1)} %pad_maximum_fusion.1.mine), channel_id=1, source_target_pairs={{0,1},{1,0},{2,3},{3,2},{4,5},{5,4},{6,7},{7,6},{8,9},{9,8},{10,11... | collective-permute-start | bytes 1179656 | tf_op jit(solution)/shard_map/ppermute | solution.py:43
  25.9 11.2 %collective-permute-start.2 = (f32[3,2,64,256]{3,2,1,0:T(8,128)S(1)}, f32[3,2,64,256]{3,2,1,0:T(8,128)S(1)}, u32[]{:S(2)}, u32[]{:S(2)}) collective-permute-start(f32[3,2,64,256]{3,2,1,0:T(8,128)S(1)} %get-tuple-element.17.mine), channel_id=1, source_target_pairs={{0,1},{1,0},{2,3},{3,2},{4,5},{5,4},{6,7},{7,6},{8,9},{9,8},{10,11... | collective-permute-start | bytes 1179656 | tf_op jit(solution)/shard_map/ppermute | solution.py:43
  26.8 10.3 %collective-permute-start.8 = (f32[3,2,64,256]{3,2,1,0:T(8,128)S(1)}, f32[3,2,64,256]{3,2,1,0:T(8,128)S(1)}, u32[]{:S(2)}, u32[]{:S(2)}) collective-permute-start(f32[3,2,64,256]{3,2,1,0:T(8,128)S(1)} %collective-permute-done.7.rest_0_), channel_id=1, source_target_pairs={{0,1},{1,0},{2,3},{3,2},{4,5},{5,4},{6,7},{7,6},{8,9},{9,8},{10,11... | collective-permute-start | bytes 1179656 | tf_op jit(solution)/shard_map/ppermute | solution.py:43
  26.8 5.9 %collective-permute-start.9 = (f32[2,2,64,128]{3,2,1,0:T(8,128)S(1)}, f32[2,2,64,128]{3,2,1,0:T(8,128)S(1)}, u32[]{:S(2)}, u32[]{:S(2)}) collective-permute-start(f32[2,2,64,128]{3,2,1,0:T(8,128)S(1)} %collective-permute-done.4), channel_id=1, source_target_pairs={{0,2},{2,0},{1,3},{3,1},{4,6},{6,4},{5,7},{7,5},{8,10},{10,8},{9,1... | collective-permute-start | bytes 393224 | tf_op jit(solution)/shard_map/ppermute | solution.py:43
  32.7 4.4 %collective-permute-start.10 = (f32[1,2,2,64,128]{4,3,2,1,0:T(8,128)S(1)}, f32[1,2,2,64,128]{4,3,2,1,0:T(8,128)S(1)}, u32[]{:S(2)}, u32[]{:S(2)}) collective-permute-start(f32[1,2,2,64,128]{4,3,2,1,0:T(8,128)S(1)} %bitcast.18), channel_id=1, source_target_pairs={{0,1},{1,0},{2,3},{3,2},{4,5},{5,4},{6,7},{7,6},{8,9},{9,8},{10,11... | collective-permute-start | bytes 393224 | tf_op jit(solution)/shard_map/ppermute | solution.py:43
